TPU v7x, 256 devices: a whole 4x4x8 slice. The times are simulated.
256 devices in a mesh: seq: 64 (over x_hi, y, z), tp: 4 (over x_lo, core).
Axes of the slice: x: 4 (x_hi: 2, x_lo: 2; x = x_hi * 2 + x_lo), y: 4, z: 8, core: 2. Of those that a mesh axis runs over, the one named last changes fastest.
Arguments:
- features: bfloat16 [16384, 3, 4096], P('seq', None, 'tp'), may hold values from -6 to 6
- short_taps: float32 [3, 7, 4096], P(None, None, 'tp'), may hold values from -2 to 2
- residue: float32 [16, 4096], P(None, 'tp'), may hold values from -1.5 to 1.5
- decay_rate: float32 [16, 4096], P(None, 'tp'), may hold values from 6.1035157e-06 to 0.05
- w_out: bfloat16 [4096, 4096], P('tp', 'seq'), may hold values from -0.09375 to 0.09375
- cotangent: bfloat16 [16384, 4096], P('seq', 'tp'), may hold values from -16 to 16
Outputs:
- mixed: bfloat16 [16384, 4096], P('seq', 'tp')
- grad_features: bfloat16 [16384, 3, 4096], P('seq', None, 'tp')
- grad_weight: float32 [4096, 4096], P('tp', 'seq')
- grad_taps: float32 [3, 7, 4096], P(None, None, 'tp')
- grad_residue: float32 [16, 4096], P(None, 'tp')
- grad_log_rate: float32 [16, 4096], P(None, 'tp')
All inputs are finite; a program needn't handle non-finite values.
Results may differ from a plain program's by a relative error of at most 0.013.
Values may be sent and summed in bfloat16 or wider, within the bound.
No kernel may reach another device: no remote copies, remote signals or barrier semaphores. Data moves between devices by JAX's collectives and lax.ppermute only.
A program may use at most 128 MiB of HBM per device.

v0:
```python
import jax
import jax.numpy as jnp
from jax import lax
from jax.sharding import PartitionSpec as P


def shifted(array, axis, by):
    devices = lax.axis_size(axis)
    pairs = [(i, i + by) for i in range(devices) if 0 <= i + by < devices]
    return lax.ppermute(array, axis, pairs)


def pair_combine(earlier, later):
    return (earlier[0] * later[0], later[0] * earlier[1] + later[1])


def decay_prefix(values, rate_row):
    channels, length = values.shape
    block_len = min(128, length)
    block_count = length // block_len
    offsets = jnp.arange(block_len, dtype=jnp.float32)
    rising = jnp.exp(rate_row[:, None] * offsets[None, :])
    falling = jnp.exp(-rate_row[:, None] * offsets[None, :])
    shaped = values.reshape(channels, block_count, block_len) * rising[:, None, :]
    triangle = (offsets[:, None] <= offsets[None, :]).astype(jnp.float32)
    summed = jnp.einsum("cqs,st->cqt", shaped, triangle, precision=lax.Precision.HIGHEST)
    inside = summed * falling[:, None, :]
    factor = jnp.broadcast_to(jnp.exp(-rate_row * block_len)[:, None], (channels, block_count))
    _, running = lax.associative_scan(pair_combine, (factor, inside[:, :, -1]), axis=1)
    entering = jnp.concatenate([jnp.zeros((channels, 1), jnp.float32), running[:, :-1]], axis=1)
    carried = entering[:, :, None] * jnp.exp(
        -rate_row[:, None, None] * (offsets[None, None, :] + 1.0)
    )
    return (inside + carried).reshape(channels, length)


def modal_output(signal, rates, coeffs, starts):
    length = signal.shape[1]
    offsets = jnp.arange(length, dtype=jnp.float32)

    def one_mode(running_sum, params):
        rate_row, coeff_row, start_row = params
        states = decay_prefix(signal, rate_row) + start_row[:, None] * jnp.exp(
            -rate_row[:, None] * (offsets[None, :] + 1.0)
        )
        return (running_sum + coeff_row[:, None] * states, states)

    result, states_all = lax.scan(one_mode, jnp.zeros_like(signal), (rates, coeffs, starts))
    return (result, states_all)


def modal_grads(states_all, upstream, rates, coeffs, starts, finals):
    length = upstream.shape[1]
    offsets = jnp.arange(length, dtype=jnp.float32)

    def one_mode(running_sum, params):
        rate_row, coeff_row, start_row, final_row, states = params
        adjoint = jnp.flip(decay_prefix(jnp.flip(upstream, 1), rate_row), 1)
        adjoint = adjoint + final_row[:, None] * jnp.exp(
            -rate_row[:, None] * (length - offsets[None, :])
        )
        previous = jnp.concatenate([start_row[:, None], states[:, :-1]], axis=1)
        sums_pair = (jnp.sum(upstream * states, axis=1), jnp.sum(adjoint * previous, axis=1))
        return (running_sum + coeff_row[:, None] * adjoint, sums_pair)

    result, (alpha_rows, beta_rows) = lax.scan(
        one_mode, jnp.zeros_like(upstream), (rates, coeffs, starts, finals, states_all)
    )
    return (result, alpha_rows, beta_rows)


def coef_grads(alpha_rows, beta_rows, rates, residue):
    scales = jnp.sqrt(-jnp.expm1(-2.0 * rates))
    grad_res = scales * alpha_rows
    grad_log = rates * (
        alpha_rows * residue * jnp.exp(-2.0 * rates) / scales
        - jnp.exp(-rates) * residue * scales * beta_rows
    )
    return (grad_res, grad_log)


def local(features, short_taps, residue, decay_rate, w_out, cotangent):
    tok_count = features.shape[0]
    tap_reach = short_taps.shape[1] - 1
    earlier = shifted(features[tok_count - tap_reach :], "seq", 1)
    extended = jnp.concatenate([earlier, features], axis=0)
    mixed_in = short_taps[:, 0, :] * features
    for tap_index in range(1, tap_reach + 1):
        mixed_in = (
            mixed_in
            + short_taps[:, tap_index, :]
            * extended[tap_reach - tap_index : tap_reach - tap_index + tok_count]
        )
    query_part = mixed_in[:, 0, :]
    keyed = mixed_in[:, 1, :]
    valued = mixed_in[:, 2, :]
    product = (keyed * valued).astype(jnp.bfloat16)
    coeffs = residue * jnp.sqrt(-jnp.expm1(-2.0 * decay_rate))
    mode_count = residue.shape[0]
    chan_share = product.shape[1] // lax.axis_size("seq")
    first_channel = lax.axis_index("seq") * chan_share
    local_rates = lax.dynamic_slice_in_dim(decay_rate, first_channel, chan_share, 1)
    local_coeffs = lax.dynamic_slice_in_dim(coeffs, first_channel, chan_share, 1)
    local_residue = lax.dynamic_slice_in_dim(residue, first_channel, chan_share, 1)
    empty_state = jnp.zeros((mode_count, chan_share), jnp.float32)
    by_channel = lax.all_to_all(product.T, "seq", split_axis=0, concat_axis=1, tiled=True).astype(
        jnp.float32
    )
    conv_channels, mode_states = modal_output(by_channel, local_rates, local_coeffs, empty_state)
    convolved = lax.all_to_all(
        conv_channels.astype(jnp.bfloat16), "seq", split_axis=1, concat_axis=0, tiled=True
    ).T
    gated = (query_part * convolved).astype(jnp.bfloat16)
    full_weight = lax.all_gather(w_out, "seq", axis=1, tiled=True)
    partial_out = jnp.dot(gated, full_weight, preferred_element_type=jnp.float32)
    mixed = lax.psum_scatter(
        partial_out.astype(jnp.bfloat16), "tp", scatter_dimension=1, tiled=True
    )
    grad_rows = lax.all_gather(cotangent, "tp", axis=1, tiled=True)
    grad_gated = lax.dot_general(
        grad_rows, full_weight, (((1,), (1,)), ((), ())), preferred_element_type=jnp.float32
    ).astype(jnp.bfloat16)
    weight_term = lax.dot_general(
        gated, grad_rows, (((0,), (0,)), ((), ())), preferred_element_type=jnp.float32
    )
    grad_weight = lax.psum_scatter(weight_term, "seq", scatter_dimension=1, tiled=True)
    grad_conv = (grad_gated * query_part).astype(jnp.bfloat16)
    grad_channels = lax.all_to_all(
        grad_conv.T, "seq", split_axis=0, concat_axis=1, tiled=True
    ).astype(jnp.float32)
    back_channels, alpha_rows, beta_rows = modal_grads(
        mode_states, grad_channels, local_rates, local_coeffs, empty_state, empty_state
    )
    grad_product = lax.all_to_all(
        back_channels.astype(jnp.bfloat16), "seq", split_axis=1, concat_axis=0, tiled=True
    ).T
    local_res, local_log = coef_grads(alpha_rows, beta_rows, local_rates, local_residue)
    grad_residue, grad_log_rate = (
        lax.all_gather(local_res, "seq", axis=1, tiled=True),
        lax.all_gather(local_log, "seq", axis=1, tiled=True),
    )
    grad_query = grad_gated * convolved
    grad_key = (grad_product * valued).astype(jnp.bfloat16)
    grad_value = (grad_product * keyed).astype(jnp.bfloat16)
    grad_mixed_in = jnp.stack([grad_query, grad_key, grad_value], axis=1)
    later_rows = shifted(grad_mixed_in[:tap_reach], "seq", -1)
    grad_ext = jnp.concatenate([grad_mixed_in, later_rows], axis=0)
    grad_feat = short_taps[:, 0, :] * grad_mixed_in
    tap_terms = [
        jnp.einsum("tjc,tjc->jc", grad_mixed_in, features, preferred_element_type=jnp.float32)
    ]
    for tap_index in range(1, tap_reach + 1):
        grad_feat = (
            grad_feat + short_taps[:, tap_index, :] * grad_ext[tap_index : tap_index + tok_count]
        )
        tap_terms.append(
            jnp.einsum(
                "tjc,tjc->jc",
                grad_mixed_in,
                extended[tap_reach - tap_index : tap_reach - tap_index + tok_count],
                preferred_element_type=jnp.float32,
            )
        )
    tap_local = jnp.stack(tap_terms, axis=1)
    grad_taps = lax.psum(tap_local, "seq")
    return (
        mixed,
        grad_feat.astype(jnp.bfloat16),
        grad_weight,
        grad_taps,
        grad_residue,
        grad_log_rate,
    )


def solution(mesh):
    return jax.shard_map(
        local,
        mesh=mesh,
        in_specs=(
            P("seq", None, "tp"),
            P(None, None, "tp"),
            P(None, "tp"),
            P(None, "tp"),
            P("tp", "seq"),
            P("seq", "tp"),
        ),
        out_specs=(
            P("seq", "tp"),
            P("seq", None, "tp"),
            P("tp", "seq"),
            P(None, None, "tp"),
            P(None, "tp"),
            P(None, "tp"),
        ),
        check_vma=False,
    )
```

profile of v0, /device:TPU:32, one launch (start us, length us, event | category | flops | bytes accessed | tf_op | source)
XLA Modules:
  0.0 2031.8 jit_solution(4164407407298874918)
XLA Ops:
  15.5 7.8 multiply_add_fusion.15
  23.2 20.7 %all-gather.5.cloned.1.call-done = bf16[256,4096]{1,0:T(8,128)(2,1)} async-done(((bf16[256,1024]{1,0:T(8,128)(2,1)}), bf16[256,4096]{1,0:T(8,128)(2,1)}) %all-gather.5.cloned.1.call-update) | async-done | bytes 2097168 | tf_op jit(solution)/shard_map/all_gather | solution.py:119
  43.9 155.4 %all-gather.3.cloned.1.call-done = bf16[1024,4096]{0,1:T(8,128)(2,1)} async-done(((bf16[1024,64]{0,1:T(8,128)(2,1)}), bf16[1024,4096]{0,1:T(8,128)(2,1)}) %all-gather.3.cloned.1.call-update) | async-done | bytes 8388624 | tf_op jit(solution)/shard_map/all_gather | solution.py:114
  209.1 8.0 all-to-all-start
  220.1 14.6 all-to-all-done
  240.4 183.7 %while.30 = (s32[]{:T(128)}, f32[16,16384]{1,0:T(8,128)}, f32[16,16,16384]{2,1,0:T(8,128)}, f32[16,16]{1,0:T(8,128)S(1)}, f32[16,16384]{1,0:T(8,128)S(1)}, /*ind...) while((s32[]{:T(128)}, f32[16,16384]{1,0:T(8,128)}, ...), condition=%wide.region_1.2_spmd.clone.clone, body=%wide.region_0.1_spmd.clone.clone.sunk | while | flops 406116288 | bytes 18331572 | solution.py:48
  426.2 13.3 all-to-all-start.1
  440.8 509.2 %while.29 = (s32[]{:T(128)}, f32[16,16384]{1,0:T(8,128)}, f32[16,16]{1,0:T(8,128)S(1)}, f32[16,16]{1,0:T(8,128)S(1)}, f32[16,16]{1,0:T(8,128)S(1)}, /*index=5*/f...) while((s32[]{:T(128)}, f32[16,16384]{1,0:T(8,128)}, ...), condition=%wide.region_6.7_spmd.clone, body=%wide.region_3.0_spmd.clone.sunk | while | flops 406378432 | bytes 24557768 | solution.py:66
  443.2 9.2 rev.11
  460.2 9.2 rev.12
  474.7 9.2 rev.11
  491.7 9.2 rev.12
  506.6 9.2 rev.11
  523.5 9.2 rev.12
  538.4 9.2 rev.11
  555.4 9.2 rev.12
  570.3 9.2 rev.11
  587.2 9.2 rev.12
  602.1 9.2 rev.11
  619.1 9.2 rev.12
  633.9 9.2 rev.11
  650.9 9.2 rev.12
  665.8 9.2 rev.11
  682.8 9.2 rev.12
  697.6 9.2 rev.11
  714.6 9.2 rev.12
  729.5 9.2 rev.11
  746.5 9.2 rev.12
  761.3 9.2 rev.11
  778.3 9.2 rev.12
  793.2 9.2 rev.11
  810.1 9.2 rev.12
  825.0 9.2 rev.11
  842.0 9.2 rev.12
  856.8 9.2 rev.11
  873.8 9.2 rev.12
  888.7 9.2 rev.11
  905.7 9.2 rev.12
  920.5 9.2 rev.11
  937.5 9.2 rev.12
  952.1 13.3 all-to-all-start.3
  967.5 13.7 all-to-all-done.3
  1000.4 9.9 fusion.47
  1014.5 176.0 %all_gather.14 = f32[16,1024]{0,1:T(8,128)S(1)} all-gather(f32[16,16]{0,1:T(8,128)S(1)} %get-tuple-element.307), channel_id=1, replica_groups=mesh['seq'=64,'tp'=4] {'seq'}, dimensions={1}, use_global_device_ids=true | all-gather | bytes 66560 | tf_op jit(solution)/shard_map/all_gather | solution.py:139
  1191.4 180.4 %all_gather.15 = f32[16,1024]{0,1:T(8,128)S(1)} all-gather(f32[16,16]{0,1:T(8,128)S(1)} %get-tuple-element.306), channel_id=1, replica_groups=mesh['seq'=64,'tp'=4] {'seq'}, dimensions={1}, use_global_device_ids=true | all-gather | bytes 66560 | tf_op jit(solution)/shard_map/all_gather | solution.py:140
  1376.5 218.9 %all-reduce.33.cloned.1.call-done = f32[3,7,1024]{2,0,1:T(4,128)} async-done(((f32[3,7,1024]{2,0,1:T(4,128)}), f32[3,7,1024]{2,0,1:T(4,128)}) %all-reduce.33.cloned.1.call-update) | async-done | bytes 86032 | tf_op jit(solution)/shard_map/psum | solution.py:165
  1596.9 28.9 %reduce-scatter.3.cloned.1.call-done = bf16[256,1024]{1,0:T(8,128)(2,1)} async-done(((bf16[256,4096]{1,0:T(8,128)(2,1)}), bf16[256,1024]{1,0:T(8,128)(2,1)}) %reduce-scatter.3.cloned.1.call-update) | async-done | bytes 524304 | tf_op jit(solution)/shard_map/reduce_scatter | solution.py:116
  1625.9 399.4 %reduce-scatter.5.cloned.1.call-done = f32[1024,64]{0,1:T(8,128)} async-done(((f32[1024,4096]{0,1:T(8,128)}), f32[1024,64]{0,1:T(8,128)}) %reduce-scatter.5.cloned.1.call-update) | async-done | bytes 262160 | tf_op jit(solution)/shard_map/reduce_scatter | solution.py:126
  (2525 shorter events, 456.3 us)
Async XLA Ops:
  7.2 36.8 %all-gather.5.cloned.1.call-start = ((), (), s32[]{:S(2)}) async-start(), calls=%async_computation.8 | async-start | bytes 2621440 | tf_op jit(solution)/shard_map/all_gather | solution.py:119
  7.9 191.4 %all-gather.3.cloned.1.call-start = ((), (), s32[]{:S(2)}) async-start(), calls=%async_computation.6 | async-start | bytes 8519680 | tf_op jit(solution)/shard_map/all_gather | solution.py:114
  9.5 6.0 collective-permute-start
  23.2 182.4 %copy-start = (f32[256,3,1024]{2,0,1:T(8,128)}, f32[256,3,1024]{2,0,1:T(8,128)S(1)}, u32[]{:S(2)}) copy-start(f32[256,3,1024]{2,0,1:T(8,128)S(1)} %multiply_add_fusion.15) | copy-start | bytes 9437188
  205.7 1.4 copy-start.10
  209.1 25.5 %all-to-all-start = ((bf16[64,16,256]{2,1,0:T(8,128)(2,1)}), bf16[64,16,256]{2,1,0:T(8,128)(2,1)S(1)}, u32[]{:S(2)}, u32[]{:S(2)}) async-start(bf16[64,16,256]{2,1,0:T(8,128)(2,1)} %bitcast.18), calls=%async_computation | async-start | bytes 1048576 | tf_op jit(solution)/shard_map/all_to_all | solution.py:106
  234.6 191.6 %all-to-all-start.2 = ((bf16[64,16,256]{2,1,0:T(8,128)(2,1)}), bf16[64,16,256]{2,1,0:T(8,128)(2,1)}, u32[]{:S(2)}, u32[]{:S(2)}) async-start(bf16[64,16,256]{2,1,0:T(8,128)(2,1)} %bitcast.25), calls=%async_computation.3 | async-start | bytes 1048576 | tf_op jit(solution)/shard_map/all_to_all | solution.py:128
  426.2 525.9 %all-to-all-start.1 = ((bf16[16,64,256]{2,0,1:T(8,128)(2,1)}), bf16[16,64,256]{2,0,1:T(8,128)(2,1)}, u32[]{:S(2)}, u32[]{:S(2)}) async-start(bf16[16,64,256]{2,0,1:T(8,128)(2,1)} %bitcast.189), calls=%async_computation.1 | async-start | bytes 1048576 | tf_op jit(solution)/shard_map/all_to_all | solution.py:110
  952.1 33.8 %copy-start.1 = (f32[256,3,1024]{2,0,1:T(8,128)S(1)}, f32[256,3,1024]{2,0,1:T(8,128)}, u32[]{:S(2)}) copy-start(f32[256,3,1024]{2,0,1:T(8,128)} %copy-done) | copy-start | bytes 9437188
  952.1 29.1 %all-to-all-start.3 = ((bf16[16,64,256]{2,0,1:T(8,128)(2,1)}), bf16[16,64,256]{2,0,1:T(8,128)(2,1)}, u32[]{:S(2)}, u32[]{:S(2)}) async-start(bf16[16,64,256]{2,0,1:T(8,128)(2,1)} %bitcast.291), calls=%async_computation.4 | async-start | bytes 1048576 | tf_op jit(solution)/shard_map/all_to_all | solution.py:134
  965.4 630.0 %all-reduce.33.cloned.1.call-start = ((), (), s32[]{:S(2)}) async-start(), calls=%async_computation.10 | async-start | bytes 229376 | tf_op jit(solution)/shard_map/psum | solution.py:165
  985.9 1.8 copy-start.9
  985.9 1.8 copy-start.11
  985.9 2.8 copy-start.8
  987.7 4.2 copy-start.4
  987.7 4.2 copy-start.6
  987.8 0.9 copy-start.2
  992.0 0.6 copy-start.12
  992.7 633.1 %reduce-scatter.3.cloned.1.call-start = ((), (), s32[]{:S(2)}) async-start(), calls=%async_computation.7 | async-start | bytes 2621440 | tf_op jit(solution)/shard_map/reduce_scatter | solution.py:116
  1000.1 1025.2 %reduce-scatter.5.cloned.1.call-start = ((), (), s32[]{:S(2)}) async-start(), calls=%async_computation.9 | async-start | bytes 17039360 | tf_op jit(solution)/shard_map/reduce_scatter | solution.py:126
  1010.3 1.0 copy-start.3
  1010.3 1.2 copy-start.5
  1010.3 1.4 copy-start.7
  1011.8 360.7 %collective-permute-start.1 = (bf16[6,3,1024]{2,0,1:T(8,128)(2,1)S(1)}, bf16[6,3,1024]{2,0,1:T(8,128)(2,1)S(1)}, u32[]{:S(2)}, u32[]{:S(2)}) collective-permute-start(bf16[6,3,1024]{2,0,1:T(8,128)(2,1)S(1)} %slice.600), channel_id=1, source_target_pairs={{4,0},{8,4},{12,8},{16,12},{20,16},{24,20},{28,24},{32,28},{36,32}... | collective-permute-start | bytes 110600 | tf_op jit(solution)/shard_map/ppermute | solution.py:10
Sparse Core Ops, SparseCore 0:
  9.8 34.0 all-gather.4
  47.7 151.6 all-gather.2
  992.8 602.4 all-reduce.32
  1598.5 27.3 reduce-scatter.2
  1628.8 396.4 reduce-scatter.4
where the time goes:
time: 2040 us; the launch traced here: 2030 us
  waiting for transfers between devices  854 us (42%)
  local copies, waits for them, and re-layouts  456 us (22%)
  blocking collectives  356 us (17%)
  other arithmetic  252 us (12%)
  starting transfers between devices  47 us (2%)
  matrix products  45.4 us (2%)
    reduce_scatter x1, waiting for transfers between devices, local(): lax.psum_scatter(weight_term, 'seq', scatter_dimension=1, tiled=True)  399 us
    rev x32, local copies, waits for them, and re-layouts, one_mode(): adjoint = jnp.flip(decay_prefix(jnp.flip(upstream, 1), rate_row), 1)  294 us
    psum x1, waiting for transfers between devices, local(): grad_taps = lax.psum(tap_local, 'seq')  219 us
    all_gather x1, blocking collectives, local(): lax.all_gather(local_log, 'seq', axis=1, tiled=True)  180 us
    all_gather x1, blocking collectives, local(): lax.all_gather(local_res, 'seq', axis=1, tiled=True)  176 us
    all_gather x1, waiting for transfers between devices, local(): full_weight = lax.all_gather(w_out, 'seq', axis=1, tiled=True)  155 us
    slice x544, local copies, waits for them, and re-layouts, decay_prefix(): lax.associative_scan(pair_combine, (factor, inside[:, :, -1]), axis=1)  63.4 us
    reduce_sum x16, other arithmetic, one_mode(): jnp.sum(adjoint * previous, axis=1)  48.7 us
  transfers between devices with their start and end apart: 11, of which 8 were waited for; matrix products, arithmetic and copies ran while one was open for 36% of the time, Pallas kernels for 0%

commit v1 on v0

v1 whole, which is shorter than its diff:
```python
import jax
import jax.numpy as jnp
from jax import lax
from jax.experimental import pallas as pl
from jax.experimental.pallas import tpu as pltpu
from jax.sharding import Mesh, PartitionSpec as P

F32 = jnp.float32
BF16 = jnp.bfloat16
SEQ = ("xh", "y", "z")
NX, NY, NZ = 2, 4, 8
SLABS = NX * NY * NZ
SUB = 8
LANES = 128
GROUPS = 1
HIGH = dict(exponent_bits=8, mantissa_bits=7)


def spread(row):
    return jnp.broadcast_to(row, (SUB, LANES))


def sub_index():
    return lax.broadcasted_iota(jnp.int32, (SUB, LANES), 0)


def earlier_sum(ends, decay):
    index = sub_index()

    def moved(value, by):
        return jnp.where(index >= by, pltpu.roll(value, by, 0), 0.0)

    total = moved(ends, 1)
    factor = decay
    for by in (1, 2, 4):
        total = total + factor * moved(total, by)
        factor = factor * factor
    return total


def later_sum(ends, decay):
    index = sub_index()

    def moved(value, by):
        return jnp.where(index < SUB - by, pltpu.roll(value, SUB - by, 0), 0.0)

    total = moved(ends, 1)
    factor = decay
    for by in (1, 2, 4):
        total = total + factor * moved(total, by)
        factor = factor * factor
    return total


def lane_groups(run):
    def kernel(*refs):
        width = refs[0].shape[1]
        for group in range(width // LANES):
            column = pl.program_id(0) * (width // LANES) + group
            run(pl.ds(group * LANES, LANES), column, *refs)

    return kernel


def decays(rate_ref, lanes, modes):
    return [spread(jnp.exp(-rate_ref[m : m + 1, lanes])) for m in modes]


def local_states_kernel(backward, lanes, column, signal_ref, rate_ref, end_ref, enter_ref):
    modes = rate_ref.shape[0]
    steps = signal_ref.shape[0] // SUB
    decay = decays(rate_ref, lanes, range(modes))

    def step(i, states):
        at = steps - 1 - i if backward else i
        value = signal_ref[pl.ds(at, SUB, stride=steps), lanes]
        return tuple(decay[m] * states[m] + value for m in range(modes))

    zero = jnp.zeros((SUB, LANES), F32)
    states = lax.fori_loop(0, steps, step, (zero,) * modes, unroll=8)
    index = sub_index().astype(F32)
    distance = index if backward else (SUB - 1.0) - index
    for m in range(modes):
        rate = spread(rate_ref[m : m + 1, lanes]) * steps
        weighted = jnp.exp(-rate * distance) * states[m]
        end_ref[m, pl.ds(column, 1), :] = jnp.sum(weighted, axis=0, keepdims=True)
        join = later_sum if backward else earlier_sum
        enter_ref[m, :, lanes] = join(states[m], jnp.exp(-rate))


def start_states(lanes, column, rate_ref, enter_ref, outer_ref, steps, backward, m):
    index = sub_index().astype(F32)
    distance = (SUB - 1.0) - index if backward else index
    rate = spread(rate_ref[m : m + 1, lanes]) * steps
    outer = spread(outer_ref[m, pl.ds(column, 1), :])
    return enter_ref[m, :, lanes] + jnp.exp(-rate * distance) * outer


def output_steps(backward, lanes, signal_ref, decay, coeff, start, out_ref):
    steps = signal_ref.shape[0] // SUB
    modes = len(decay)

    def step(i, states):
        at = steps - 1 - i if backward else i
        value = signal_ref[pl.ds(at, SUB, stride=steps), lanes]
        states = tuple(decay[m] * states[m] + value for m in range(modes))
        terms = [coeff[m] * states[m] for m in range(modes)]
        while len(terms) > 1:
            terms = [terms[j] + terms[j + 1] for j in range(0, len(terms), 2)]
        out_ref[pl.ds(at, SUB, stride=steps), lanes] = terms[0]
        return states

    lax.fori_loop(0, steps, step, start, unroll=4)


def forward_kernel(lanes, column, signal_ref, rate_ref, coeff_ref, enter_ref, outer_ref, out_ref):
    modes = rate_ref.shape[0]
    steps = signal_ref.shape[0] // SUB
    decay = decays(rate_ref, lanes, range(modes))
    coeff = [spread(coeff_ref[m : m + 1, lanes]) for m in range(modes)]
    start = tuple(
        start_states(lanes, column, rate_ref, enter_ref, outer_ref, steps, False, m) for m in range(modes)
    )
    output_steps(False, lanes, signal_ref, decay, coeff, start, out_ref)


def backward_kernel(
    lanes,
    column,
    signal_ref,
    rate_ref,
    coeff_ref,
    enter_ref,
    outer_ref,
    slope_ref,
    partial_ref,
    out_ref,
    beta_ref,
):
    modes = rate_ref.shape[0]
    steps = signal_ref.shape[0] // SUB
    decay = decays(rate_ref, lanes, range(modes))
    coeff = [spread(coeff_ref[m : m + 1, lanes]) for m in range(modes)]
    start = tuple(
        start_states(lanes, column, rate_ref, enter_ref, outer_ref, steps, True, m) for m in range(modes)
    )
    for m in range(modes):
        crossing = jnp.sum(decay[m] * slope_ref[m, :, lanes] * start[m], axis=0, keepdims=True)
        beta_ref[m, pl.ds(column, 1), :] = partial_ref[m, pl.ds(column, 1), :] + crossing
    output_steps(True, lanes, signal_ref, decay, coeff, start, out_ref)


def sums_kernel(
    lanes, column, signal_ref, grad_ref, rate_ref, enter_ref, outer_ref, alpha_ref, partial_ref, slope_ref
):
    modes = rate_ref.shape[0]
    steps = signal_ref.shape[0] // SUB
    zero = jnp.zeros((SUB, LANES), F32)
    group = 8
    for first in range(0, modes, group):
        decay = decays(rate_ref, lanes, range(first, first + group))
        start = tuple(
            start_states(lanes, column, rate_ref, enter_ref, outer_ref, steps, False, first + m)
            for m in range(group)
        )

        def step(i, carry):
            states, slopes, alphas, betas = carry
            value = signal_ref[pl.ds(i, SUB, stride=steps), lanes]
            grad = grad_ref[pl.ds(i, SUB, stride=steps), lanes]
            slopes = tuple(decay[m] * slopes[m] + states[m] for m in range(group))
            states = tuple(decay[m] * states[m] + value for m in range(group))
            alphas = tuple(alphas[m] + grad * states[m] for m in range(group))
            betas = tuple(betas[m] + grad * slopes[m] for m in range(group))
            return states, slopes, alphas, betas

        zeros = (zero,) * group
        _, slopes, alphas, betas = lax.fori_loop(0, steps, step, (start, zeros, zeros, zeros), unroll=4)
        for m in range(group):
            row = first + m
            alpha_ref[row, pl.ds(column, 1), :] = jnp.sum(alphas[m], axis=0, keepdims=True)
            partial_ref[row, pl.ds(column, 1), :] = jnp.sum(betas[m], axis=0, keepdims=True)
            slope_ref[row, :, lanes] = slopes[m]


def modal_call(body, name, work, inputs, outputs):
    tokens, channels = inputs[0][1].shape
    modes = inputs[-1][1].shape[0]
    block = LANES * GROUPS
    blocks = {
        "tokens": pl.BlockSpec((tokens, block), lambda c: (0, c)),
        "modes": pl.BlockSpec((modes, block), lambda c: (0, c)),
        "subs": pl.BlockSpec((modes, SUB, block), lambda c: (0, 0, c)),
        "rows": pl.BlockSpec((modes, channels // LANES, LANES), lambda c: (0, 0, 0)),
    }
    shapes = {
        "tokens": (tokens, channels),
        "subs": (modes, SUB, channels),
        "rows": (modes, channels // LANES, LANES),
    }
    return pl.pallas_call(
        lane_groups(body),
        name=name,
        grid=(channels // block,),
        in_specs=[blocks[kind] for kind, _ in inputs],
        out_specs=[blocks[kind] for kind in outputs],
        out_shape=[jax.ShapeDtypeStruct(shapes[kind], F32) for kind in outputs],
        cost_estimate=pl.CostEstimate(
            flops=work * modes * tokens * channels, transcendentals=0, bytes_accessed=8 * tokens * channels
        ),
    )(*[array for _, array in inputs])


def local_states(signal, rates, backward):
    return modal_call(
        lambda *refs: local_states_kernel(backward, *refs),
        "adjoint_ends" if backward else "state_ends",
        2,
        [("tokens", signal), ("modes", rates)],
        ["rows", "subs"],
    )


def forward_output(signal, rates, coeffs, enter, outer):
    inputs = [("tokens", signal), ("modes", rates), ("modes", coeffs), ("subs", enter), ("rows", outer)]
    return modal_call(forward_kernel, "modal_forward", 4, inputs, ["tokens"])[0]


def backward_output(signal, rates, coeffs, enter, outer, slopes, partial):
    inputs = [("tokens", signal), ("modes", rates), ("modes", coeffs), ("subs", enter), ("rows", outer)]
    inputs += [("subs", slopes), ("rows", partial)]
    return modal_call(backward_kernel, "modal_backward", 4, inputs, ["tokens", "rows"])


def mode_sums(signal, grads, rates, enter, outer):
    inputs = [("tokens", signal), ("tokens", grads), ("modes", rates), ("subs", enter), ("rows", outer)]
    return modal_call(sums_kernel, "mode_sums", 8, inputs, ["rows", "rows", "subs"])


def slab_scan_kernel(backward, ends_ref, decay_ref, out_ref):
    decay = decay_ref[...]
    state = jnp.zeros(decay.shape, F32)
    order = range(SLABS - 1, -1, -1) if backward else range(SLABS)
    for slab in order:
        out_ref[slab] = state
        state = decay * state + ends_ref[slab]


def entering(ends, slab_decay, backward, beside):
    shape = (SLABS, ends.size // SLABS // LANES, LANES)
    mine = lax.axis_index(SEQ)
    decay = lax.dynamic_index_in_dim(slab_decay.reshape(shape), mine, 0, keepdims=False)
    gathered = lax.all_to_all(ends.reshape(shape), SEQ, 0, 0, tiled=True)
    gathered, beside = lax.optimization_barrier((gathered, beside))
    scanned = pl.pallas_call(
        lambda *refs: slab_scan_kernel(backward, *refs),
        name="slab_scan_back" if backward else "slab_scan",
        out_shape=jax.ShapeDtypeStruct(shape, F32),
        cost_estimate=pl.CostEstimate(
            flops=2 * ends.size, transcendentals=0, bytes_accessed=8 * ends.size
        ),
    )(gathered, decay)
    outer = lax.all_to_all(scanned, SEQ, 0, 0, tiled=True).reshape(ends.shape)
    return outer, beside


def ring(array, axis, size, by):
    return lax.ppermute(array, axis, [(i, (i + by) % size) for i in range(size)])


def gather_weight(w_rows):
    other = ring(w_rows, "xh", NX, 1)
    first = lax.axis_index("xh") == 0
    pair = jnp.concatenate([jnp.where(first, w_rows, other), jnp.where(first, other, w_rows)], axis=0)
    return lax.all_gather(pair, ("y", "z"), axis=0, tiled=True)


def to_gather_order(rows):
    tokens, width = rows.shape
    cols = width // SLABS
    return rows.reshape(tokens, NX, NY * NZ, cols).transpose(0, 2, 1, 3).reshape(tokens, width)


def from_gather_order(rows):
    tokens, width = rows.shape
    cols = width // SLABS
    return rows.reshape(tokens, NY * NZ, NX, cols).transpose(0, 2, 1, 3).reshape(tokens, width)


def gather_columns(block):
    size = lax.axis_size("tp")
    width = block.shape[1]
    own = lax.axis_index("tp")
    whole = jnp.zeros((block.shape[0], size * width), block.dtype)
    for offset in range(size):
        part = ring(block, "tp", size, -offset) if offset else block
        whole = lax.dynamic_update_slice_in_dim(whole, part, (own + offset) % size * width, 1)
    return whole


def shifted(array, by):
    pairs = [(i, i + by) for i in range(SLABS) if 0 <= i + by < SLABS]
    return lax.ppermute(array, SEQ, pairs)


def to_ring_order(rows):
    tokens, width = rows.shape
    cols = width // SLABS
    return rows.reshape(tokens, NX * NY, NZ, cols).transpose(0, 2, 1, 3).reshape(tokens, width)


def weight_grad(term):
    cols, channels = term.shape[0] // SLABS, term.shape[1]
    summed = lax.psum_scatter(term, "z", scatter_dimension=0, tiled=True)
    by_y = summed.reshape(NX, NY, cols, channels)
    own = lax.axis_index("y")

    def block(target):
        return lax.dynamic_index_in_dim(by_y, target % NY, 1, keepdims=False)

    total = block(own).astype(F32)
    for offset in range(1, NY):
        total = total + ring(block(own - offset), "y", NY, -offset).astype(F32)
    mine = lax.axis_index("xh")
    away = ring(lax.dynamic_index_in_dim(total, 1 - mine, 0, keepdims=False), "xh", NX, 1)
    return (lax.dynamic_index_in_dim(total, mine, 0, keepdims=False) + away).T


def total_over_slabs(rows):
    count, channels = rows.shape
    shape = (SLABS, count * channels // SLABS // LANES, LANES)
    pieces = lax.all_to_all(rows.reshape(shape), SEQ, 0, 0, tiled=True)
    summed = jnp.sum(pieces, axis=0)
    copies = jnp.broadcast_to(summed[None], shape)
    return lax.all_to_all(copies, SEQ, 0, 0, tiled=True).reshape(count, channels)


def local(features, short_taps, residue, decay_rate, w_out, cotangent):
    tok_count = features.shape[0]
    modes, channels = residue.shape
    taps = short_taps.shape[1]
    tap_reach = taps - 1

    earlier = shifted(features[tok_count - tap_reach :], 1)
    weight = gather_weight(w_out.T)

    extended = jnp.concatenate([earlier, features], axis=0)
    mixed_in = short_taps[:, 0, :] * features
    for tap in range(1, taps):
        mixed_in = mixed_in + short_taps[:, tap, :] * extended[tap_reach - tap : tap_reach - tap + tok_count]
    query_part, keyed, valued = mixed_in[:, 0, :], mixed_in[:, 1, :], mixed_in[:, 2, :]
    product = lax.reduce_precision(keyed * valued, **HIGH)
    scales = jnp.sqrt(-jnp.expm1(-2.0 * decay_rate))
    coeffs = residue * scales
    slab_decay = jnp.exp(-decay_rate * tok_count)

    state_ends, state_enter = local_states(product, decay_rate, False)
    state_ends, cot_block = lax.optimization_barrier((state_ends, cotangent))
    cot_rows = gather_columns(cot_block)
    state_outer, cot_rows = entering(state_ends, slab_decay, False, cot_rows)
    cot_order, cot_ring = to_gather_order(cot_rows), to_ring_order(cot_rows)
    state_outer, cot_order, cot_ring = lax.optimization_barrier((state_outer, cot_order, cot_ring))
    convolved = forward_output(product, decay_rate, coeffs, state_enter, state_outer).astype(BF16)
    gated = (query_part * convolved).astype(BF16)
    weight_term = lax.dot_general(cot_ring, gated, (((0,), (0,)), ((), ())), preferred_element_type=F32)
    weight, weight_term = lax.optimization_barrier((weight, weight_term.astype(BF16)))
    grad_weight = weight_grad(weight_term)

    grad_gated = lax.reduce_precision(jnp.dot(cot_order, weight, preferred_element_type=F32), **HIGH)
    grad_conv = lax.reduce_precision(grad_gated * query_part, **HIGH)
    adj_ends, adj_enter = local_states(grad_conv, decay_rate, True)
    sums_here = mode_sums(product, grad_conv, decay_rate, state_enter, state_outer)
    adj_outer, (sums_here, gated) = entering(adj_ends, slab_decay, True, (sums_here, gated))
    alpha_rows, beta_part, slopes = sums_here
    partial_out = lax.dot_general(gated, weight, (((1,), (1,)), ((), ())), preferred_element_type=F32)
    partial_out = from_gather_order(partial_out.astype(BF16))
    adj_outer, partial_out = lax.optimization_barrier((adj_outer, partial_out))
    mixed = lax.psum_scatter(partial_out, "tp", scatter_dimension=1, tiled=True)
    grad_product, beta_rows = backward_output(
        grad_conv, decay_rate, coeffs, adj_enter, adj_outer, slopes, beta_part
    )
    grad_product = grad_product.astype(BF16)

    grad_query = (grad_gated * convolved).astype(BF16)
    grad_key = (grad_product * valued).astype(BF16)
    grad_value = (grad_product * keyed).astype(BF16)
    grad_mixed_in = jnp.stack([grad_query, grad_key, grad_value], axis=1)
    later = shifted(grad_mixed_in[:tap_reach], -1)
    grad_ext = jnp.concatenate([grad_mixed_in, later], axis=0)
    grad_feat = short_taps[:, 0, :] * grad_mixed_in
    tap_terms = []
    for tap in range(taps):
        if tap:
            grad_feat = grad_feat + short_taps[:, tap, :] * grad_ext[tap : tap + tok_count]
        tap_terms.append(
            jnp.einsum(
                "tjc,tjc->jc",
                grad_mixed_in,
                extended[tap_reach - tap : tap_reach - tap + tok_count],
                preferred_element_type=F32,
            )
        )
    tap_rows = jnp.stack(tap_terms, axis=1).reshape(3 * taps, channels)
    spare = jnp.zeros((SLABS - 2 * modes - 3 * taps, channels), F32)
    sums = total_over_slabs(jnp.concatenate([alpha_rows.reshape(modes, channels), beta_rows.reshape(modes, channels), tap_rows, spare], axis=0))
    alpha_sum, beta_sum = sums[:modes], sums[modes : 2 * modes]
    grad_taps = sums[2 * modes : 2 * modes + 3 * taps].reshape(3, taps, channels)
    grad_residue = scales * alpha_sum
    grad_log_rate = decay_rate * (
        alpha_sum * residue * jnp.exp(-2.0 * decay_rate) / scales - jnp.exp(-decay_rate) * coeffs * beta_sum
    )
    return (mixed, grad_feat.astype(BF16), grad_weight, grad_taps, grad_residue, grad_log_rate)


def solution(mesh):
    parts = Mesh(mesh.devices.reshape(NX, NY, NZ, mesh.devices.shape[1]), ("xh", "y", "z", "tp"))
    return jax.shard_map(
        local,
        mesh=parts,
        in_specs=(
            P(SEQ, None, "tp"),
            P(None, None, "tp"),
            P(None, "tp"),
            P(None, "tp"),
            P("tp", SEQ),
            P(SEQ, "tp"),
        ),
        out_specs=(
            P(SEQ, "tp"),
            P(SEQ, None, "tp"),
            P("tp", SEQ),
            P(None, None, "tp"),
            P(None, "tp"),
            P(None, "tp"),
        ),
        check_vma=False,
    )
```

time: 2040 us -> 273 us (0.13)
  waiting for transfers between devices: 854 us -> 42.3 us
  local copies, waits for them, and re-layouts: 456 us -> 36.3 us
  blocking collectives: 356 us -> 0 us
  other arithmetic: 252 us -> 27.7 us
  starting transfers between devices: 47 us -> 88.8 us
  Pallas kernels: 0 us -> 40.1 us
  matrix products: 45.4 us -> 20.7 us
    reduce_scatter x2, waiting for transfers between devices: 428 us -> 0.02 us  [the longest x1 0.02 us: weight_grad(): summed = lax.psum_scatter(term, 'z', scatter_dimension=0, tiled=True)]
    all_gather x2 -> x0, blocking collectives: 356 us -> none  [the longest x1 180 us: local(): lax.all_gather(local_log, 'seq', axis=1, tiled=True)]
    rev x32 -> x0, local copies, waits for them, and re-layouts: 294 us -> none  [one_mode(): adjoint = jnp.flip(decay_prefix(jnp.flip(upstream, 1), rate_row), 1)]
    psum x1 -> x0, waiting for transfers between devices: 219 us -> none  [local(): grad_taps = lax.psum(tap_local, 'seq')]
    all_gather x2 -> x1, waiting for transfers between devices: 176 us -> 1.91 us  [gather_weight(): return lax.all_gather(pair, ('y', 'z'), axis=0, tiled=True)]
    add x705 -> x2, other arithmetic: 97.6 us -> 8.41 us  [the longest x1 7.3 us: local(): mixed_in + short_taps[:, tap, :] * extended[tap_reach - tap:tap_reach - t...]
    reduce_sum x32 -> x1, other arithmetic: 87.2 us -> 0.07 us  [total_over_slabs(): summed = jnp.sum(pieces, axis=0)]
    slice x610 -> x4, local copies, waits for them, and re-layouts: 71 us -> 0.84 us  [the longest x1 0.82 us: local(): earlier = shifted(features[tok_count - tap_reach:], 1)]
  transfers between devices with their start and end apart: 11 -> 19, of which waited for: 8 -> 11; matrix products, arithmetic and copies ran while one was open for 36% -> 29% of each run, Pallas kernels for 0% -> 15%
where the time goes in v1:
time: 273 us; the launch traced here: 270 us
  starting transfers between devices  88.8 us (33%)
  waiting for transfers between devices  42.3 us (15%)
  Pallas kernels  40.1 us (15%)
  local copies, waits for them, and re-layouts  36.3 us (13%)
  other arithmetic  27.7 us (10%)
  matrix products  20.7 us (8%)
  between operations  14.3 us (5%)
    pallas_call x5, Pallas kernels, modal_call(): pl.pallas_call(lane_groups(body), name=name, grid=(channels // block,), i...  36.9 us
    all_to_all x2, starting transfers between devices, entering(): gathered = lax.all_to_all(ends.reshape(shape), SEQ, 0, 0, tiled=True)  26 us
    all_to_all x2, starting transfers between devices, entering(): outer = lax.all_to_all(scanned, SEQ, 0, 0, tiled=True).reshape(ends.shape)  25.4 us
    ppermute x8, waiting for transfers between devices, ring(): lax.ppermute(array, axis, [(i, (i + by) % size) for i in range(size)])  18.8 us
    all_to_all x1, starting transfers between devices, total_over_slabs(): pieces = lax.all_to_all(rows.reshape(shape), SEQ, 0, 0, tiled=True)  13.1 us
    ppermute x8, starting transfers between devices, ring(): lax.ppermute(array, axis, [(i, (i + by) % size) for i in range(size)])  12.1 us
    dot_general x1, matrix products, local(): jnp.dot(cot_order, weight, preferred_element_type=F32)  7.77 us
    dynamic_update_slice x4, local copies, waits for them, and re-layouts, gather_columns(): lax.dynamic_update_slice_in_dim(whole, part, (own + offset) % size * widt...  7.51 us
  transfers between devices with their start and end apart: 19, of which 11 were waited for; matrix products, arithmetic and copies ran while one was open for 29% of the time, Pallas kernels for 15%

profile of v1, /device:TPU:32, one launch (start us, length us, event | category | flops | bytes accessed | tf_op | source)
XLA Modules:
  0.0 270.2 jit_solution(8384437618357359832)
XLA Ops:
  7.2 3.1 %collective-permute-start.4 = (bf16[64,1024]{1,0:T(8,128)(2,1)}, bf16[64,1024]{1,0:T(8,128)(2,1)S(1)}, u32[]{:S(2)}, u32[]{:S(2)}) collective-permute-start(bf16[64,1024]{1,0:T(8,128)(2,1)} %bitcast.148), channel_id=1, source_target_pairs={{0,128},{128,0},{1,129},{129,1},{2,130},{130,2},{3,131},{131,3},{4... | collective-permute-start | bytes 393224 | tf_op jit(solution)/shard_map/ppermute | solution.py:268
  10.3 3.9 %collective-permute-done.4 = bf16[64,1024]{1,0:T(8,128)(2,1)S(1)} collective-permute-done((bf16[64,1024]{1,0:T(8,128)(2,1)}, bf16[64,1024]{1,0:T(8,128)(2,1)S(1)}, u32[]{:S(2)}, u32[]{:S(2)}) %collective-permute-start.4) | collective-permute-done | bytes 131104 | tf_op jit(solution)/shard_map/ppermute | solution.py:268
  16.7 3.8 %collective-permute-start = (bf16[6,3,1024]{2,0,1:T(8,128)(2,1)S(1)}, bf16[6,3,1024]{2,0,1:T(8,128)(2,1)S(1)}, u32[]{:S(2)}, u32[]{:S(2)}) collective-permute-start(bf16[6,3,1024]{2,0,1:T(8,128)(2,1)S(1)} %slice.103), channel_id=1, source_target_pairs={{0,4},{4,8},{8,12},{12,16},{16,20},{20,24},{24,28},{28,32},{32,36}... | collective-permute-start | bytes 110600 | tf_op jit(solution)/shard_map/ppermute | solution.py:303
  20.6 1.5 fusion.30
  22.7 7.3 %multiply_add_fusion = f32[256,3,1024]{2,0,1:T(8,128)S(1)} fusion(bf16[256,3,1024]{2,0,1:T(8,128)(2,1)} %param.6, bf16[6,3,1024]{2,0,1:T(8,128)(2,1)S(1)} %collective-permute-done, f32[3,1024]{1,0:T(4,128)S(1)} %get-tuple-element.95, f32[3,1024]{1,0:T(4,128)S(1)} %get-tuple-element.96, f32[3,1024]{1,0:T(4,128)S(1)} %get-tuple-element.97, ...), kind=kLoop, calls=%fused_computation.22 | loop fusion | flops 29884416 | bytes 4841472 | tf_op jit(solution)/shard_map/add | solution.py:350
  31.2 6.2 %state_ends.1 = (f32[16,8,128]{2,1,0:T(8,128)}, f32[16,8,1024]{2,1,0:T(8,128)}) custom-call(f32[256,1024]{1,0:T(8,128)} %multiply_reduce-precision_fusion.1.refs_0_, f32[16,1024]{1,0:T(8,128)} %refs_1_.7), custom_call_target="tpu_custom_call" | custom-call | flops 8388608 | bytes 2097152 | tf_op jit(solution)/shard_map/state_ends/pallas_call | solution.py:201
  37.4 2.1 copy.13
  42.6 15.1 %all-to-all-start = ((f32[64,2,128]{2,1,0:T(2,128)}), f32[64,2,128]{2,1,0:T(2,128)S(1)}, u32[]{:S(2)}, u32[]{:S(2)}) async-start(f32[64,2,128]{2,1,0:T(2,128)} %bitcast.149), calls=%async_computation | async-start | bytes 131072 | tf_op jit(solution)/shard_map/all_to_all | solution.py:253
  57.7 1.5 broadcast_in_dim.12
  59.3 1.9 constant_dynamic-update-slice_fusion.3
  61.1 1.9 constant_dynamic-update-slice_fusion.2
  63.0 2.8 %collective-permute-done.2 = bf16[256,1024]{0,1:T(8,128)(2,1)} collective-permute-done((bf16[256,1024]{0,1:T(8,128)(2,1)}, bf16[256,1024]{0,1:T(8,128)(2,1)}, u32[]{:S(2)}, u32[]{:S(2)}) %collective-permute-start.2) | collective-permute-done | bytes 524320 | tf_op jit(solution)/shard_map/ppermute | solution.py:268
  65.8 1.9 constant_dynamic-update-slice_fusion.1
  67.7 1.9 constant_dynamic-update-slice_fusion
  70.3 1.6 slab_scan.1
  71.9 15.0 %all-to-all-start.1 = ((f32[64,2,128]{2,1,0:T(2,128)}), f32[64,2,128]{2,1,0:T(2,128)S(1)}, u32[]{:S(2)}, u32[]{:S(2)}) async-start(f32[64,2,128]{2,1,0:T(2,128)} %slab_scan.1), calls=%async_computation.1 | async-start | bytes 131072 | tf_op jit(solution)/shard_map/all_to_all | solution.py:263
  87.1 3.2 %copy.17 = bf16[256,32,2,64]{0,3,2,1:T(8,128)(2,1)} copy(bf16[256,32,2,64]{0,3,1,2:T(8,128)(2,1)} %bitcast.20) | data formatting | bytes 4194304 | tf_op jit(solution)/shard_map/transpose | solution.py:281
  90.3 3.3 %copy.18 = bf16[256,8,8,64]{0,3,2,1:T(8,128)(2,1)} copy(bf16[256,8,8,64]{0,3,1,2:T(8,128)(2,1)} %bitcast.23) | data formatting | bytes 4194304 | tf_op jit(solution)/shard_map/transpose | solution.py:309
  93.6 5.1 %all-to-all-done.1 = f32[64,2,128]{2,1,0:T(2,128)S(1)} async-done(((f32[64,2,128]{2,1,0:T(2,128)}), f32[64,2,128]{2,1,0:T(2,128)S(1)}, u32[]{:S(2)}, u32[]{:S(2)}) %all-to-all-start.1) | async-done | bytes 65568 | tf_op jit(solution)/shard_map/all_to_all | solution.py:263
  99.3 7.2 %modal_forward.1 = f32[256,1024]{1,0:T(8,128)} custom-call(f32[256,1024]{1,0:T(8,128)} %multiply_reduce-precision_fusion.1.refs_0_, f32[16,1024]{1,0:T(8,128)} %refs_1_.7, f32[16,1024]{1,0:T(8,128)} %get-tuple-element.93.refs_2_, f32[16,8,1024]{2,1,0:T(8,128)} %get-tuple-element.38.refs_3_, f32[16,8,128]{2,1,0:T(8,128)} %bitcast.141), custom_call_target="tpu_custom_call" | custom-call | flops 16777216 | bytes 2097152 | tf_op jit(solution)/shard_map/modal_forward/pallas_call | solution.py:201
  108.9 5.6 %convolution_convert_fusion = bf16[4096,1024]{1,0:T(8,128)(2,1)} fusion(bf16[256,4096]{0,1:T(8,128)(2,1)S(1)} %bitcast.136, bf16[256,1024]{1,0:T(8,128)(2,1)S(1)} %fusion.13), kind=kOutput, calls=%fused_computation.7 | convolution fusion | flops 2151677952 | bytes 11010048 | tf_op jit(solution)/shard_map/dot_general | solution.py:365
  114.5 1.9 all-gather.2.cloned.1.call-done
  116.4 7.8 %fusion.19 = (bf16[256,1,1024]{2,0,1:T(8,128)(2,1)}, f32[256,1024]{1,0:T(8,128)}) fusion(f32[256,1024]{1,0:T(8,128)} %modal_forward.1, f32[256,3,1024]{2,0,1:T(8,128)S(1)} %multiply_add_fusion, bf16[256,4096]{0,1:T(8,128)(2,1)} %bitcast.135, bf16[4096,1024]{1,0:T(8,128)(2,1)} %all-gather.2.cloned.1.call-done), kind=kOutput, calls=%fused_computation.48 | convolution fusion | flops 2149318656 | bytes 14155776 | tf_op jit(solution)/shard_map/dot_general | solution.py:369
  124.2 6.3 %adjoint_ends.1 = (f32[16,8,128]{2,1,0:T(8,128)}, f32[16,8,1024]{2,1,0:T(8,128)}) custom-call(f32[256,1024]{1,0:T(8,128)} %get-tuple-element.79.refs_0_.refs_1_, f32[16,1024]{1,0:T(8,128)} %refs_1_.7), custom_call_target="tpu_custom_call" | custom-call | flops 8388608 | bytes 2097152 | tf_op jit(solution)/shard_map/adjoint_ends/pallas_call | solution.py:201
  130.5 10.9 %all-to-all-start.2 = ((f32[64,2,128]{2,1,0:T(2,128)}), f32[64,2,128]{2,1,0:T(2,128)S(1)}, u32[]{:S(2)}, u32[]{:S(2)}) async-start(f32[64,2,128]{2,1,0:T(2,128)} %bitcast.150), calls=%async_computation.2 | async-start | bytes 131072 | tf_op jit(solution)/shard_map/all_to_all | solution.py:253
  141.3 9.6 %mode_sums.1 = (f32[16,8,128]{2,1,0:T(8,128)}, f32[16,8,128]{2,1,0:T(8,128)}, f32[16,8,1024]{2,1,0:T(8,128)}) custom-call(f32[256,1024]{1,0:T(8,128)} %multiply_reduce-precision_fusion.1.refs_0_, f32[256,1024]{1,0:T(8,128)} %get-tuple-element.79.refs_0_.refs_1_, f32[16,1024]{1,0:T(8,128)} %refs_1_.7, f32[16,8,1024]{2,1,0:T(8,128)} %get-tuple-element.38.refs_3_, ...), custom_call_target="tpu_custom_call" | custom-call | flops 33554432 | bytes 2097152 | tf_op jit(solution)/shard_map/mode_sums/pallas_call | solution.py:201
  150.9 2.4 all-to-all-done.2.refs_0_
  154.0 1.6 slab_scan_back.1
  155.6 10.4 %all-to-all-start.3 = ((f32[64,2,128]{2,1,0:T(2,128)}), f32[64,2,128]{2,1,0:T(2,128)S(1)}, u32[]{:S(2)}, u32[]{:S(2)}) async-start(f32[64,2,128]{2,1,0:T(2,128)} %slab_scan_back.1), calls=%async_computation.3 | async-start | bytes 131072 | tf_op jit(solution)/shard_map/all_to_all | solution.py:263
  166.0 7.3 %convolution_convert_fusion.1 = bf16[256,4096]{1,0:T(8,128)(2,1)} fusion(bf16[256,1024]{1,0:T(8,128)(2,1)} %copy-done.10, bf16[4096,1024]{1,0:T(8,128)(2,1)} %all-gather.2.cloned.1.call-done), kind=kOutput, calls=%fused_computation.8 | convolution fusion | flops 2148532224 | bytes 11010048 | tf_op jit(solution)/shard_map/dot_general | solution.py:375
  173.3 4.1 %copy.19 = bf16[256,4096]{0,1:T(8,128)(2,1)} copy(bf16[256,4096]{1,0:T(8,128)(2,1)} %convolution_convert_fusion.1) | data formatting | bytes 4194304 | tf_op jit(solution)/shard_map/convert_element_type | solution.py:376
  177.4 3.3 %copy.20 = bf16[256,2,32,64]{0,3,2,1:T(8,128)(2,1)} copy(bf16[256,2,32,64]{0,3,1,2:T(8,128)(2,1)} %bitcast.138) | data formatting | bytes 4194304 | tf_op jit(solution)/shard_map/transpose | solution.py:287
  181.3 7.6 %modal_backward.1 = (f32[256,1024]{1,0:T(8,128)}, f32[16,8,128]{2,1,0:T(8,128)}) custom-call(f32[256,1024]{1,0:T(8,128)} %get-tuple-element.79.refs_0_.refs_1_, f32[16,1024]{1,0:T(8,128)} %refs_1_.7, f32[16,1024]{1,0:T(8,128)} %get-tuple-element.93.refs_2_, f32[16,8,1024]{2,1,0:T(8,128)} %get-tuple-element.48.refs_3_, f32[16,8,128]{2,1,0:T(8,128)} %bitcast.143, ...), custom_call_target="tpu_custom_call" | custom-call | flops 16777216 | bytes 2097152 | tf_op jit(solution)/shard_map/modal_backward/pallas_call | solution.py:201
  189.0 1.8 fusion.18
  190.9 3.2 %fusion.5 = (f32[3,1024]{1,0:T(4,128)S(1)}, f32[3,1024]{1,0:T(4,128)S(1)}, f32[3,1024]{1,0:T(4,128)S(1)}, f32[3,1024]{1,0:T(4,128)S(1)}, f32[3,1024]{1,0:T(4,128...) fusion(bf16[256,3,1024]{2,0,1:T(8,128)(2,1)S(1)} %copy-done.7, bf16[6,3,1024]{2,0,1:T(8,128)(2,1)S(1)} %collective-permute-done, ...), kind=kLoop, calls=%fused_computation.19 | loop fusion | flops 40872960 | bytes 3268608 | tf_op jit(solution)/shard_map/tjc,tjc->jc/dot_general | solution.py:396
  195.3 13.1 %all-to-all-start.4 = ((f32[64,8,128]{2,1,0:T(8,128)}), f32[64,8,128]{2,1,0:T(8,128)S(1)}, u32[]{:S(2)}, u32[]{:S(2)}) async-start(f32[64,8,128]{2,1,0:T(8,128)} %maximum_maximum_fusion), calls=%async_computation.6 | async-start | bytes 524288 | tf_op jit(solution)/shard_map/all_to_all | solution.py:332
  209.8 2.3 collective-permute-start.5
  212.2 6.8 %collective-permute-done.5 = bf16[6,3,1024]{2,0,1:T(8,128)(2,1)S(1)} collective-permute-done((bf16[6,3,1024]{2,0,1:T(8,128)(2,1)S(1)}, bf16[6,3,1024]{2,0,1:T(8,128)(2,1)S(1)}, u32[]{:S(2)}, u32[]{:S(2)}) %collective-permute-start.5) | collective-permute-done | bytes 36896 | tf_op jit(solution)/shard_map/ppermute | solution.py:303
  219.2 6.7 %all-to-all-done.4 = f32[64,8,128]{2,1,0:T(8,128)S(1)} async-done(((f32[64,8,128]{2,1,0:T(8,128)}), f32[64,8,128]{2,1,0:T(8,128)S(1)}, u32[]{:S(2)}, u32[]{:S(2)}) %all-to-all-start.4) | async-done | bytes 262176 | tf_op jit(solution)/shard_map/all_to_all | solution.py:332
  226.6 5.8 %all-to-all-start.5 = ((f32[64,8,128]{2,1,0:T(8,128)}), f32[64,8,128]{2,1,0:T(8,128)S(1)}, u32[]{:S(2)}, u32[]{:S(2)}) async-start(f32[64,8,128]{2,1,0:T(8,128)} %broadcast_in_dim.14), calls=%async_computation.7 | async-start | bytes 524288 | tf_op jit(solution)/shard_map/all_to_all | solution.py:335
  233.7 2.8 %collective-permute-start.6 = (bf16[2,64,1024]{2,1,0:T(8,128)(2,1)S(1)}, bf16[2,64,1024]{2,1,0:T(8,128)(2,1)S(1)}, u32[]{:S(2)}, u32[]{:S(2)}) collective-permute-start(bf16[2,64,1024]{2,1,0:T(8,128)(2,1)S(1)} %get-tuple-element.75), channel_id=1, source_target_pairs={{0,96},{32,0},{64,32},{96,64},{1,97},{33,1},{65,33},{97,65},{2,98}... | collective-permute-start | bytes 786440 | tf_op jit(solution)/shard_map/ppermute | solution.py:268
  238.2 4.5 %add_convert_fusion = bf16[256,3,1024]{2,0,1:T(8,128)(2,1)} fusion(bf16[262,3,1024]{2,0,1:T(8,128)(2,1)S(1)} %pad_maximum_fusion, f32[3,1024]{1,0:T(4,128)} %copy-done.16, f32[3,1024]{1,0:T(4,128)} %copy-done.17, f32[3,1024]{1,0:T(4,128)} %copy-done.18, f32[3,1024]{1,0:T(4,128)} %copy-done.19, f32[3,1024]{1,0:T(4,128)S(1)} %get-tuple-element.99, ...), kind=kLoop, calls=%fused_computation.21 | loop fusion | flops 18087936 | bytes 12668928 | tf_op jit(solution)/shard_map/convert_element_type | solution.py:412
  242.7 6.0 %collective-permute-done.6 = bf16[2,64,1024]{2,1,0:T(8,128)(2,1)S(1)} collective-permute-done((bf16[2,64,1024]{2,1,0:T(8,128)(2,1)S(1)}, bf16[2,64,1024]{2,1,0:T(8,128)(2,1)S(1)}, u32[]{:S(2)}, u32[]{:S(2)}) %collective-permute-start.6) | collective-permute-done | bytes 262176 | tf_op jit(solution)/shard_map/ppermute | solution.py:268
  248.7 3.3 %collective-permute-done.8 = bf16[2,64,1024]{2,1,0:T(8,128)(2,1)S(1)} collective-permute-done((bf16[2,64,1024]{2,1,0:T(8,128)(2,1)S(1)}, bf16[2,64,1024]{2,1,0:T(8,128)(2,1)S(1)}, u32[]{:S(2)}, u32[]{:S(2)}) %collective-permute-start.8) | collective-permute-done | bytes 262176 | tf_op jit(solution)/shard_map/ppermute | solution.py:268
  253.2 2.8 %collective-permute-start.9 = (f32[64,1024]{1,0:T(8,128)S(1)}, f32[64,1024]{1,0:T(8,128)S(1)}, u32[]{:S(2)}, u32[]{:S(2)}) collective-permute-start(f32[64,1024]{1,0:T(8,128)S(1)} %dynamic-slice_bitcast_fusion), channel_id=1, source_target_pairs={{0,128},{128,0},{1,129},{129,1},{2,130},{130,2},{3,131},{131,3},{4... | collective-permute-start | bytes 786440 | tf_op jit(solution)/shard_map/ppermute | solution.py:268
  256.6 1.6 fusion.24
  258.2 2.0 copy.21
  260.2 2.7 collective-permute-done.9
  (102 shorter events, 21.4 us)
Async XLA Ops:
  7.2 109.2 %all-gather.2.cloned.1.call-start = ((), (), s32[]{:S(2)}) async-start(), calls=%async_computation.8 | async-start | bytes 8650752 | tf_op jit(solution)/shard_map/all_gather | solution.py:275
  7.2 7.0 %collective-permute-start.4 = (bf16[64,1024]{1,0:T(8,128)(2,1)}, bf16[64,1024]{1,0:T(8,128)(2,1)S(1)}, u32[]{:S(2)}, u32[]{:S(2)}) collective-permute-start(bf16[64,1024]{1,0:T(8,128)(2,1)} %bitcast.148), channel_id=1, source_target_pairs={{0,128},{128,0},{1,129},{129,1},{2,130},{130,2},{3,131},{131,3},{4... | collective-permute-start | bytes 393224 | tf_op jit(solution)/shard_map/ppermute | solution.py:268
  16.7 6.0 %collective-permute-start = (bf16[6,3,1024]{2,0,1:T(8,128)(2,1)S(1)}, bf16[6,3,1024]{2,0,1:T(8,128)(2,1)S(1)}, u32[]{:S(2)}, u32[]{:S(2)}) collective-permute-start(bf16[6,3,1024]{2,0,1:T(8,128)(2,1)S(1)} %slice.103), channel_id=1, source_target_pairs={{0,4},{4,8},{8,12},{12,16},{16,20},{20,24},{24,28},{28,32},{32,36}... | collective-permute-start | bytes 110600 | tf_op jit(solution)/shard_map/ppermute | solution.py:303
  22.1 9.1 %copy-start.16 = (f32[3,1024]{1,0:T(4,128)}, f32[3,1024]{1,0:T(4,128)S(1)}, u32[]{:S(2)}) copy-start(f32[3,1024]{1,0:T(4,128)S(1)} %get-tuple-element.95) | copy-start | bytes 36868
  22.1 9.1 %copy-start.17 = (f32[3,1024]{1,0:T(4,128)}, f32[3,1024]{1,0:T(4,128)S(1)}, u32[]{:S(2)}) copy-start(f32[3,1024]{1,0:T(4,128)S(1)} %get-tuple-element.96) | copy-start | bytes 36868
  22.2 9.0 %copy-start.18 = (f32[3,1024]{1,0:T(4,128)}, f32[3,1024]{1,0:T(4,128)S(1)}, u32[]{:S(2)}) copy-start(f32[3,1024]{1,0:T(4,128)S(1)} %get-tuple-element.97) | copy-start | bytes 36868
  22.2 9.0 %copy-start.19 = (f32[3,1024]{1,0:T(4,128)}, f32[3,1024]{1,0:T(4,128)S(1)}, u32[]{:S(2)}) copy-start(f32[3,1024]{1,0:T(4,128)S(1)} %get-tuple-element.98) | copy-start | bytes 36868
  22.2 9.0 %copy-start.20 = (f32[3,1,1024]{2,0,1:T(4,128)}, f32[3,1,1024]{2,0,1:T(4,128)S(1)}, u32[]{:S(2)}) copy-start(f32[3,1,1024]{2,0,1:T(4,128)S(1)} %copy.90) | copy-start | bytes 36868
  30.0 11.2 %copy-start.8 = (f32[16,1024]{1,0:T(8,128)S(1)}, f32[16,1024]{1,0:T(8,128)}, u32[]{:S(2)}) copy-start(f32[16,1024]{1,0:T(8,128)} %refs_1_.7) | copy-start | bytes 196612
  30.1 11.2 %copy-start.15 = (f32[16,1024]{1,0:T(8,128)S(1)}, f32[16,1024]{1,0:T(8,128)}, u32[]{:S(2)}) copy-start(f32[16,1024]{1,0:T(8,128)} %param.8) | copy-start | bytes 196612
  39.5 21.6 %collective-permute-start.1 = (bf16[256,1024]{0,1:T(8,128)(2,1)}, bf16[256,1024]{0,1:T(8,128)(2,1)}, u32[]{:S(2)}, u32[]{:S(2)}) collective-permute-start(bf16[256,1024]{0,1:T(8,128)(2,1)} %copy.13), channel_id=1, source_target_pairs={{0,3},{1,0},{2,1},{3,2},{4,7},{5,4},{6,5},{7,6},{8,11},{9,8},{10,9... | collective-permute-start | bytes 1572872 | tf_op jit(solution)/shard_map/ppermute | solution.py:268
  39.5 26.4 %collective-permute-start.2 = (bf16[256,1024]{0,1:T(8,128)(2,1)}, bf16[256,1024]{0,1:T(8,128)(2,1)}, u32[]{:S(2)}, u32[]{:S(2)}) collective-permute-start(bf16[256,1024]{0,1:T(8,128)(2,1)} %copy.13), channel_id=1, source_target_pairs={{0,2},{1,3},{2,0},{3,1},{4,6},{5,7},{6,4},{7,5},{8,10},{9,11},{10,... | collective-permute-start | bytes 1572872 | tf_op jit(solution)/shard_map/ppermute | solution.py:268
  41.0 26.7 %collective-permute-start.3 = (bf16[256,1024]{0,1:T(8,128)(2,1)}, bf16[256,1024]{0,1:T(8,128)(2,1)}, u32[]{:S(2)}, u32[]{:S(2)}) collective-permute-start(bf16[256,1024]{0,1:T(8,128)(2,1)} %copy.13), channel_id=1, source_target_pairs={{0,1},{1,2},{2,3},{3,0},{4,5},{5,6},{6,7},{7,4},{8,9},{9,10},{10,1... | collective-permute-start | bytes 1572872 | tf_op jit(solution)/shard_map/ppermute | solution.py:268
  42.6 27.0 %all-to-all-start = ((f32[64,2,128]{2,1,0:T(2,128)}), f32[64,2,128]{2,1,0:T(2,128)S(1)}, u32[]{:S(2)}, u32[]{:S(2)}) async-start(f32[64,2,128]{2,1,0:T(2,128)} %bitcast.149), calls=%async_computation | async-start | bytes 131072 | tf_op jit(solution)/shard_map/all_to_all | solution.py:253
  69.6 0.6 copy-start.13
  71.9 26.8 %all-to-all-start.1 = ((f32[64,2,128]{2,1,0:T(2,128)}), f32[64,2,128]{2,1,0:T(2,128)S(1)}, u32[]{:S(2)}, u32[]{:S(2)}) async-start(f32[64,2,128]{2,1,0:T(2,128)} %slab_scan.1), calls=%async_computation.1 | async-start | bytes 131072 | tf_op jit(solution)/shard_map/all_to_all | solution.py:263
  86.9 145.7 %reduce-scatter.5.cloned.1.call-start = ((), (), s32[]{:S(2)}) async-start(), calls=%async_computation.10 | async-start | bytes 9437184 | tf_op jit(solution)/shard_map/reduce_scatter | solution.py:314
  98.7 0.6 copy-start.11
  106.5 2.3 copy-start.6
  108.0 0.8 copy-start.10
  130.5 22.9 %all-to-all-start.2 = ((f32[64,2,128]{2,1,0:T(2,128)}), f32[64,2,128]{2,1,0:T(2,128)S(1)}, u32[]{:S(2)}, u32[]{:S(2)}) async-start(f32[64,2,128]{2,1,0:T(2,128)} %bitcast.150), calls=%async_computation.2 | async-start | bytes 131072 | tf_op jit(solution)/shard_map/all_to_all | solution.py:253
  153.4 0.6 copy-start.14
  155.6 25.1 %all-to-all-start.3 = ((f32[64,2,128]{2,1,0:T(2,128)}), f32[64,2,128]{2,1,0:T(2,128)S(1)}, u32[]{:S(2)}, u32[]{:S(2)}) async-start(f32[64,2,128]{2,1,0:T(2,128)} %slab_scan_back.1), calls=%async_computation.3 | async-start | bytes 131072 | tf_op jit(solution)/shard_map/all_to_all | solution.py:263
  166.0 92.2 %reduce-scatter.3.cloned.1.call-start = ((), (), s32[]{:S(2)}) async-start(), calls=%async_computation.9 | async-start | bytes 2621440 | tf_op jit(solution)/shard_map/reduce_scatter | solution.py:378
  180.7 0.6 copy-start.12
  188.9 1.9 copy-start
  188.9 1.9 copy-start.7
  189.0 5.5 %copy-start.21 = (f32[16,8,128]{2,1,0:T(8,128)S(1)}, f32[16,8,128]{2,1,0:T(8,128)}, u32[]{:S(2)}) copy-start(f32[16,8,128]{2,1,0:T(8,128)} %get-tuple-element.54) | copy-start | bytes 196612
  189.0 5.5 %copy-start.22 = (f32[16,8,128]{2,1,0:T(8,128)S(1)}, f32[16,8,128]{2,1,0:T(8,128)}, u32[]{:S(2)}) copy-start(f32[16,8,128]{2,1,0:T(8,128)} %get-tuple-element.55) | copy-start | bytes 196612
  190.8 3.4 %copy-start.2 = (bf16[256,1,1024]{2,0,1:T(8,128)(2,1)}, bf16[256,1,1024]{2,0,1:T(8,128)(2,1)S(1)}, u32[]{:S(2)}) copy-start(bf16[256,1,1024]{2,0,1:T(8,128)(2,1)S(1)} %get-tuple-element.69) | copy-start | bytes 1572868
  190.8 3.4 %copy-start.4 = (bf16[256,1,1024]{2,0,1:T(8,128)(2,1)}, bf16[256,1,1024]{2,0,1:T(8,128)(2,1)S(1)}, u32[]{:S(2)}) copy-start(bf16[256,1,1024]{2,0,1:T(8,128)(2,1)S(1)} %get-tuple-element.70) | copy-start | bytes 1572868
  190.8 17.6 %copy-start.1 = (bf16[256,1,1024]{2,0,1:T(8,128)(2,1)S(1)}, bf16[256,1,1024]{2,0,1:T(8,128)(2,1)}, u32[]{:S(2)}) copy-start(bf16[256,1,1024]{2,0,1:T(8,128)(2,1)} %get-tuple-element.78) | copy-start | bytes 1572868
  194.2 24.9 %copy-start.3 = (bf16[256,1,1024]{2,0,1:T(8,128)(2,1)S(1)}, bf16[256,1,1024]{2,0,1:T(8,128)(2,1)}, u32[]{:S(2)}) copy-start(bf16[256,1,1024]{2,0,1:T(8,128)(2,1)} %copy-done.2) | copy-start | bytes 1572868
  194.2 24.8 %copy-start.5 = (bf16[256,1,1024]{2,0,1:T(8,128)(2,1)S(1)}, bf16[256,1,1024]{2,0,1:T(8,128)(2,1)}, u32[]{:S(2)}) copy-start(bf16[256,1,1024]{2,0,1:T(8,128)(2,1)} %copy-done.4) | copy-start | bytes 1572868
  195.3 30.5 %all-to-all-start.4 = ((f32[64,8,128]{2,1,0:T(8,128)}), f32[64,8,128]{2,1,0:T(8,128)S(1)}, u32[]{:S(2)}, u32[]{:S(2)}) async-start(f32[64,8,128]{2,1,0:T(8,128)} %maximum_maximum_fusion), calls=%async_computation.6 | async-start | bytes 524288 | tf_op jit(solution)/shard_map/all_to_all | solution.py:332
  209.8 9.2 %collective-permute-start.5 = (bf16[6,3,1024]{2,0,1:T(8,128)(2,1)S(1)}, bf16[6,3,1024]{2,0,1:T(8,128)(2,1)S(1)}, u32[]{:S(2)}, u32[]{:S(2)}) collective-permute-start(bf16[6,3,1024]{2,0,1:T(8,128)(2,1)S(1)} %slice.143), channel_id=1, source_target_pairs={{4,0},{8,4},{12,8},{16,12},{20,16},{24,20},{28,24},{32,28},{36,32}... | collective-permute-start | bytes 110600 | tf_op jit(solution)/shard_map/ppermute | solution.py:303
  226.6 29.3 %all-to-all-start.5 = ((f32[64,8,128]{2,1,0:T(8,128)}), f32[64,8,128]{2,1,0:T(8,128)S(1)}, u32[]{:S(2)}, u32[]{:S(2)}) async-start(f32[64,8,128]{2,1,0:T(8,128)} %broadcast_in_dim.14), calls=%async_computation.7 | async-start | bytes 524288 | tf_op jit(solution)/shard_map/all_to_all | solution.py:335
  233.7 14.9 %collective-permute-start.6 = (bf16[2,64,1024]{2,1,0:T(8,128)(2,1)S(1)}, bf16[2,64,1024]{2,1,0:T(8,128)(2,1)S(1)}, u32[]{:S(2)}, u32[]{:S(2)}) collective-permute-start(bf16[2,64,1024]{2,1,0:T(8,128)(2,1)S(1)} %get-tuple-element.75), channel_id=1, source_target_pairs={{0,96},{32,0},{64,32},{96,64},{1,97},{33,1},{65,33},{97,65},{2,98}... | collective-permute-start | bytes 786440 | tf_op jit(solution)/shard_map/ppermute | solution.py:268
  236.5 12.1 %collective-permute-start.7 = (bf16[2,64,1024]{2,1,0:T(8,128)(2,1)S(1)}, bf16[2,64,1024]{2,1,0:T(8,128)(2,1)S(1)}, u32[]{:S(2)}, u32[]{:S(2)}) collective-permute-start(bf16[2,64,1024]{2,1,0:T(8,128)(2,1)S(1)} %get-tuple-element.77), channel_id=1, source_target_pairs={{0,64},{32,96},{64,0},{96,32},{1,65},{33,97},{65,1},{97,33},{2,66}... | collective-permute-start | bytes 786440 | tf_op jit(solution)/shard_map/ppermute | solution.py:268
  237.3 19.3 %copy-start.9 = (f32[16,1024]{1,0:T(8,128)S(1)}, f32[16,1024]{1,0:T(8,128)}, u32[]{:S(2)}) copy-start(f32[16,1024]{1,0:T(8,128)} %refs_1_.7) | copy-start | bytes 196612
  237.3 14.7 %collective-permute-start.8 = (bf16[2,64,1024]{2,1,0:T(8,128)(2,1)S(1)}, bf16[2,64,1024]{2,1,0:T(8,128)(2,1)S(1)}, u32[]{:S(2)}, u32[]{:S(2)}) collective-permute-start(bf16[2,64,1024]{2,1,0:T(8,128)(2,1)S(1)} %get-tuple-element.76), channel_id=1, source_target_pairs={{0,32},{32,64},{64,96},{96,0},{1,33},{33,65},{65,97},{97,1},{2,34}... | collective-permute-start | bytes 786440 | tf_op jit(solution)/shard_map/ppermute | solution.py:268
  253.2 9.8 %collective-permute-start.9 = (f32[64,1024]{1,0:T(8,128)S(1)}, f32[64,1024]{1,0:T(8,128)S(1)}, u32[]{:S(2)}, u32[]{:S(2)}) collective-permute-start(f32[64,1024]{1,0:T(8,128)S(1)} %dynamic-slice_bitcast_fusion), channel_id=1, source_target_pairs={{0,128},{128,0},{1,129},{129,1},{2,130},{130,2},{3,131},{131,3},{4... | collective-permute-start | bytes 786440 | tf_op jit(solution)/shard_map/ppermute | solution.py:268
Sparse Core Ops, SparseCore 0:
  16.0 100.2 all-gather.1
  118.9 101.1 reduce-scatter.4
  222.7 33.1 reduce-scatter.2

commit v2 on v1

--- a/solution.py
+++ b/solution.py
@@ -303,27 +303,30 @@
     return lax.ppermute(array, SEQ, pairs)
 
 
-def to_ring_order(rows):
-    tokens, width = rows.shape
-    cols = width // SLABS
-    return rows.reshape(tokens, NX * NY, NZ, cols).transpose(0, 2, 1, 3).reshape(tokens, width)
+def x_pair(cot_rows):
+    tokens, width = cot_rows.shape
+    side, cols = width // NX, width // SLABS
+    mine = lax.axis_index("xh")
+
+    def half(which):
+        columns = lax.dynamic_slice_in_dim(cot_rows, which * side, side, 1)
+        return columns.reshape(tokens, NY, NZ, cols).transpose(0, 2, 1, 3).reshape(tokens, side)
+
+    return jnp.concatenate([half(mine), ring(half(1 - mine), "xh", NX, 1)], axis=0)
 
 
 def weight_grad(term):
-    cols, channels = term.shape[0] // SLABS, term.shape[1]
     summed = lax.psum_scatter(term, "z", scatter_dimension=0, tiled=True)
-    by_y = summed.reshape(NX, NY, cols, channels)
+    by_y = summed.reshape(NY, -1, summed.shape[1])
     own = lax.axis_index("y")
 
     def block(target):
-        return lax.dynamic_index_in_dim(by_y, target % NY, 1, keepdims=False)
+        return lax.dynamic_index_in_dim(by_y, target % NY, 0, keepdims=False)
 
     total = block(own).astype(F32)
     for offset in range(1, NY):
         total = total + ring(block(own - offset), "y", NY, -offset).astype(F32)
-    mine = lax.axis_index("xh")
-    away = ring(lax.dynamic_index_in_dim(total, 1 - mine, 0, keepdims=False), "xh", NX, 1)
-    return (lax.dynamic_index_in_dim(total, mine, 0, keepdims=False) + away).T
+    return total
 
 
 def total_over_slabs(rows):
@@ -358,28 +361,32 @@
     state_ends, cot_block = lax.optimization_barrier((state_ends, cotangent))
     cot_rows = gather_columns(cot_block)
     state_outer, cot_rows = entering(state_ends, slab_decay, False, cot_rows)
-    cot_order, cot_ring = to_gather_order(cot_rows), to_ring_order(cot_rows)
-    state_outer, cot_order, cot_ring = lax.optimization_barrier((state_outer, cot_order, cot_ring))
+    cot_order, cot_pair = to_gather_order(cot_rows), x_pair(cot_rows)
+    state_outer, cot_order = lax.optimization_barrier((state_outer, cot_order))
     convolved = forward_output(product, decay_rate, coeffs, state_enter, state_outer).astype(BF16)
+    convolved, cot_pair = lax.optimization_barrier((convolved, cot_pair))
     gated = (query_part * convolved).astype(BF16)
-    weight_term = lax.dot_general(cot_ring, gated, (((0,), (0,)), ((), ())), preferred_element_type=F32)
-    weight, weight_term = lax.optimization_barrier((weight, weight_term.astype(BF16)))
-    grad_weight = weight_grad(weight_term)
-
     grad_gated = lax.reduce_precision(jnp.dot(cot_order, weight, preferred_element_type=F32), **HIGH)
     grad_conv = lax.reduce_precision(grad_gated * query_part, **HIGH)
+    grad_conv, gated = lax.optimization_barrier((grad_conv, gated))
+    gated_pair = jnp.concatenate([gated, ring(gated, "xh", NX, 1)], axis=0)
     adj_ends, adj_enter = local_states(grad_conv, decay_rate, True)
     sums_here = mode_sums(product, grad_conv, decay_rate, state_enter, state_outer)
-    adj_outer, (sums_here, gated) = entering(adj_ends, slab_decay, True, (sums_here, gated))
+    adj_ends, cot_pair = lax.optimization_barrier((adj_ends, cot_pair))
+    weight_term = lax.dot_general(cot_pair, gated_pair, (((0,), (0,)), ((), ())), preferred_element_type=F32)
+    weight_term = weight_term.astype(BF16)
+    weight_sum = weight_grad(weight_term)
+    beside = (weight_term, sums_here, gated)
+    adj_outer, (_, sums_here, gated) = entering(adj_ends, slab_decay, True, beside)
     alpha_rows, beta_part, slopes = sums_here
     partial_out = lax.dot_general(gated, weight, (((1,), (1,)), ((), ())), preferred_element_type=F32)
     partial_out = from_gather_order(partial_out.astype(BF16))
     adj_outer, partial_out = lax.optimization_barrier((adj_outer, partial_out))
-    mixed = lax.psum_scatter(partial_out, "tp", scatter_dimension=1, tiled=True)
     grad_product, beta_rows = backward_output(
         grad_conv, decay_rate, coeffs, adj_enter, adj_outer, slopes, beta_part
     )
     grad_product = grad_product.astype(BF16)
+    mixed = lax.psum_scatter(partial_out, "tp", scatter_dimension=1, tiled=True)
 
     grad_query = (grad_gated * convolved).astype(BF16)
     grad_key = (grad_product * valued).astype(BF16)
@@ -402,7 +409,9 @@
         )
     tap_rows = jnp.stack(tap_terms, axis=1).reshape(3 * taps, channels)
     spare = jnp.zeros((SLABS - 2 * modes - 3 * taps, channels), F32)
-    sums = total_over_slabs(jnp.concatenate([alpha_rows.reshape(modes, channels), beta_rows.reshape(modes, channels), tap_rows, spare], axis=0))
+    rows = jnp.concatenate([alpha_rows.reshape(modes, channels), beta_rows.reshape(modes, channels), tap_rows, spare])
+    sums, weight_sum = lax.optimization_barrier((total_over_slabs(rows), weight_sum))
+    grad_weight = weight_sum.T
     alpha_sum, beta_sum = sums[:modes], sums[modes : 2 * modes]
     grad_taps = sums[2 * modes : 2 * modes + 3 * taps].reshape(3, taps, channels)
     grad_residue = scales * alpha_sum

time: 273 us -> 273 us (level)
  waiting for transfers between devices: 42.3 us -> 32.8 us
  other arithmetic: 27.7 us -> 33.1 us
  starting transfers between devices: 88.8 us -> 92.3 us
    ppermute x8 -> x9, waiting for transfers between devices: 18.8 us -> 13.9 us  [ring(): lax.ppermute(array, axis, [(i, (i + by) % size) for i in range(size)])]
    ppermute x8 -> x9, starting transfers between devices: 12.1 us -> 15.2 us  [ring(): lax.ppermute(array, axis, [(i, (i + by) % size) for i in range(size)])]
    concatenate x0 -> x1, other arithmetic: none -> 3 us  [x_pair(): jnp.concatenate([half(mine), ring(half(1 - mine), 'xh', NX, 1)], axis=0)]
    ppermute x2, waiting for transfers between devices: 7.29 us -> 4.29 us  [shifted(): return lax.ppermute(array, SEQ, pairs)]
    dynamic_slice x0 -> x1, local copies, waits for them, and re-layouts: none -> 2.9 us  [half(): columns = lax.dynamic_slice_in_dim(cot_rows, which * side, side, 1)]
    unnamed x51 -> x38, local copies, waits for them, and re-layouts: 5.48 us -> 4.02 us
  transfers between devices with their start and end apart: 19 -> 20, of which waited for: 11 -> 9; matrix products, arithmetic and copies ran while one was open for 29% -> 26% of each run, Pallas kernels for 15% -> 15%
where the time goes in v2:
time: 273 us; the launch traced here: 271 us
  starting transfers between devices  92.3 us (34%)
  Pallas kernels  40.1 us (15%)
  local copies, waits for them, and re-layouts  38.3 us (14%)
  other arithmetic  33.1 us (12%)
  waiting for transfers between devices  32.8 us (12%)
  matrix products  19.9 us (7%)
  between operations  14.2 us (5%)
    pallas_call x5, Pallas kernels, modal_call(): pl.pallas_call(lane_groups(body), name=name, grid=(channels // block,), i...  36.9 us
    all_to_all x2, starting transfers between devices, entering(): gathered = lax.all_to_all(ends.reshape(shape), SEQ, 0, 0, tiled=True)  25.6 us
    all_to_all x2, starting transfers between devices, entering(): outer = lax.all_to_all(scanned, SEQ, 0, 0, tiled=True).reshape(ends.shape)  23.9 us
    ppermute x9, starting transfers between devices, ring(): lax.ppermute(array, axis, [(i, (i + by) % size) for i in range(size)])  15.2 us
    ppermute x9, waiting for transfers between devices, ring(): lax.ppermute(array, axis, [(i, (i + by) % size) for i in range(size)])  13.9 us
    all_to_all x1, starting transfers between devices, total_over_slabs(): pieces = lax.all_to_all(rows.reshape(shape), SEQ, 0, 0, tiled=True)  12.8 us
    all_to_all x1, starting transfers between devices, total_over_slabs(): lax.all_to_all(copies, SEQ, 0, 0, tiled=True).reshape(count, channels)  8.41 us
    dynamic_update_slice x4, local copies, waits for them, and re-layouts, gather_columns(): lax.dynamic_update_slice_in_dim(whole, part, (own + offset) % size * widt...  7.51 us
  transfers between devices with their start and end apart: 20, of which 9 were waited for; matrix products, arithmetic and copies ran while one was open for 26% of the time, Pallas kernels for 15%

profile of v2, /device:TPU:32, one launch (start us, length us, event | category | flops | bytes accessed | tf_op | source)
XLA Modules:
  0.0 270.8 jit_solution(14482639684234189769)
XLA Ops:
  7.2 3.1 %collective-permute-start.4 = (bf16[64,1024]{1,0:T(8,128)(2,1)}, bf16[64,1024]{1,0:T(8,128)(2,1)S(1)}, u32[]{:S(2)}, u32[]{:S(2)}) collective-permute-start(bf16[64,1024]{1,0:T(8,128)(2,1)} %bitcast.135), channel_id=1, source_target_pairs={{0,128},{128,0},{1,129},{129,1},{2,130},{130,2},{3,131},{131,3},{4... | collective-permute-start | bytes 393224 | tf_op jit(solution)/shard_map/ppermute | solution.py:268
  10.3 3.9 %collective-permute-done.4 = bf16[64,1024]{1,0:T(8,128)(2,1)S(1)} collective-permute-done((bf16[64,1024]{1,0:T(8,128)(2,1)}, bf16[64,1024]{1,0:T(8,128)(2,1)S(1)}, u32[]{:S(2)}, u32[]{:S(2)}) %collective-permute-start.4) | collective-permute-done | bytes 131104 | tf_op jit(solution)/shard_map/ppermute | solution.py:268
  16.7 3.8 %collective-permute-start = (bf16[6,3,1024]{2,0,1:T(8,128)(2,1)S(1)}, bf16[6,3,1024]{2,0,1:T(8,128)(2,1)S(1)}, u32[]{:S(2)}, u32[]{:S(2)}) collective-permute-start(bf16[6,3,1024]{2,0,1:T(8,128)(2,1)S(1)} %slice.96), channel_id=1, source_target_pairs={{0,4},{4,8},{8,12},{12,16},{16,20},{20,24},{24,28},{28,32},{32,36}... | collective-permute-start | bytes 110600 | tf_op jit(solution)/shard_map/ppermute | solution.py:303
  22.7 7.2 %multiply_add_fusion = f32[256,3,1024]{2,0,1:T(8,128)S(1)} fusion(bf16[256,3,1024]{2,0,1:T(8,128)(2,1)} %param.6, bf16[6,3,1024]{2,0,1:T(8,128)(2,1)S(1)} %collective-permute-done, f32[3,1024]{1,0:T(4,128)S(1)} %get-tuple-element.106, f32[3,1024]{1,0:T(4,128)S(1)} %get-tuple-element.107, f32[3,1024]{1,0:T(4,128)S(1)} %get-tuple-element.108, ...), kind=kLoop, calls=%fused_computation.22 | loop fusion | flops 29884416 | bytes 4841472 | tf_op jit(solution)/shard_map/add | solution.py:353
  31.2 6.2 %state_ends.1 = (f32[16,8,128]{2,1,0:T(8,128)}, f32[16,8,1024]{2,1,0:T(8,128)}) custom-call(f32[256,1024]{1,0:T(8,128)} %multiply_reduce-precision_fusion.1.refs_0_, f32[16,1024]{1,0:T(8,128)} %refs_1_.7), custom_call_target="tpu_custom_call" | custom-call | flops 8388608 | bytes 2097152 | tf_op jit(solution)/shard_map/state_ends/pallas_call | solution.py:201
  37.3 2.1 copy.13
  41.1 15.1 %all-to-all-start = ((f32[64,2,128]{2,1,0:T(2,128)}), f32[64,2,128]{2,1,0:T(2,128)S(1)}, u32[]{:S(2)}, u32[]{:S(2)}) async-start(f32[64,2,128]{2,1,0:T(2,128)} %bitcast.136), calls=%async_computation | async-start | bytes 131072 | tf_op jit(solution)/shard_map/all_to_all | solution.py:253
  57.8 1.9 constant_dynamic-update-slice_fusion.3
  59.7 1.9 constant_dynamic-update-slice_fusion.2
  61.5 4.2 %collective-permute-done.2 = bf16[256,1024]{0,1:T(8,128)(2,1)} collective-permute-done((bf16[256,1024]{0,1:T(8,128)(2,1)}, bf16[256,1024]{0,1:T(8,128)(2,1)}, u32[]{:S(2)}, u32[]{:S(2)}) %collective-permute-start.2) | collective-permute-done | bytes 524320 | tf_op jit(solution)/shard_map/ppermute | solution.py:268
  65.8 1.9 constant_dynamic-update-slice_fusion.1
  67.7 1.9 constant_dynamic-update-slice_fusion
  69.6 2.9 %constant_dynamic-slice_fusion.1 = (bf16[256,2048]{0,1:T(8,128)(2,1)}, bf16[256,2048]{0,1:T(8,128)(2,1)S(1)}) fusion(bf16[256,4096]{0,1:T(8,128)(2,1)} %constant_dynamic-update-slice_fusion, s32[]{:T(128)S(6)} %select_n.95, s32[]{:T(128)S(6)} %select_n.96), kind=kLoop, calls=%fused_computation.77 | loop fusion | bytes 4194312 | tf_op jit(solution)/shard_map/dynamic_slice | solution.py:312
  73.5 2.7 %collective-permute-start.5 = (bf16[256,2048]{0,1:T(8,128)(2,1)}, bf16[256,2048]{0,1:T(8,128)(2,1)}, u32[]{:S(2)}, u32[]{:S(2)}) collective-permute-start(bf16[256,2048]{0,1:T(8,128)(2,1)} %bitcast.29), channel_id=1, source_target_pairs={{0,128},{128,0},{1,129},{129,1},{2,130},{130,2},{3,131},{131,3},{4... | collective-permute-start | bytes 3145736 | tf_op jit(solution)/shard_map/ppermute | solution.py:268
  79.2 13.1 %all-to-all-start.1 = ((f32[64,2,128]{2,1,0:T(2,128)}), f32[64,2,128]{2,1,0:T(2,128)S(1)}, u32[]{:S(2)}, u32[]{:S(2)}) async-start(f32[64,2,128]{2,1,0:T(2,128)} %slab_scan.1), calls=%async_computation.1 | async-start | bytes 131072 | tf_op jit(solution)/shard_map/all_to_all | solution.py:263
  92.4 2.3 copy.18
  94.7 3.2 %copy.17 = bf16[256,32,2,64]{0,3,2,1:T(8,128)(2,1)} copy(bf16[256,32,2,64]{0,3,1,2:T(8,128)(2,1)} %bitcast.20) | data formatting | bytes 4194304 | tf_op jit(solution)/shard_map/transpose | solution.py:281
  97.9 6.3 %all-to-all-done.1 = f32[64,2,128]{2,1,0:T(2,128)S(1)} async-done(((f32[64,2,128]{2,1,0:T(2,128)}), f32[64,2,128]{2,1,0:T(2,128)S(1)}, u32[]{:S(2)}, u32[]{:S(2)}) %all-to-all-start.1) | async-done | bytes 65568 | tf_op jit(solution)/shard_map/all_to_all | solution.py:263
  104.8 7.3 %modal_forward.1 = f32[256,1024]{1,0:T(8,128)} custom-call(f32[256,1024]{1,0:T(8,128)} %multiply_reduce-precision_fusion.1.refs_0_, f32[16,1024]{1,0:T(8,128)} %refs_1_.7, f32[16,1024]{1,0:T(8,128)} %get-tuple-element.104.refs_2_, f32[16,8,1024]{2,1,0:T(8,128)} %get-tuple-element.42.refs_3_, f32[16,8,128]{2,1,0:T(8,128)} %bitcast.127), custom_call_target="tpu_custom_call" | custom-call | flops 16777216 | bytes 2097152 | tf_op jit(solution)/shard_map/modal_forward/pallas_call | solution.py:201
  112.1 2.1 convert_element_type.99
  114.2 3.0 %pad_maximum_fusion = bf16[512,2048]{0,1:T(8,128)(2,1)} fusion(bf16[256,2048]{0,1:T(8,128)(2,1)} %collective-permute-done.5, bf16[256,2048]{0,1:T(8,128)(2,1)} %bitcast.123), kind=kLoop, calls=%fused_computation.23 | loop fusion | flops 4194304 | bytes 4194304 | tf_op jit(solution)/shard_map/concatenate | solution.py:315
  117.2 6.4 %convolution_reduce-precision_fusion = f32[256,1024]{1,0:T(8,128)S(1)} fusion(bf16[256,4096]{0,1:T(8,128)(2,1)} %bitcast.118, bf16[4096,1024]{1,0:T(8,128)(2,1)} %all-gather.2.cloned.1.call-done), kind=kOutput, calls=%fused_computation.33 | convolution fusion | flops 2147745792 | bytes 11534336 | tf_op jit(solution)/shard_map/dot_general | solution.py:369
  125.1 2.6 collective-permute-start.6
  127.8 6.2 %adjoint_ends.1 = (f32[16,8,128]{2,1,0:T(8,128)}, f32[16,8,1024]{2,1,0:T(8,128)}) custom-call(f32[256,1024]{1,0:T(8,128)} %get-tuple-element.45.refs_0_.refs_1_, f32[16,1024]{1,0:T(8,128)} %refs_1_.7), custom_call_target="tpu_custom_call" | custom-call | flops 8388608 | bytes 2097152 | tf_op jit(solution)/shard_map/adjoint_ends/pallas_call | solution.py:201
  134.0 5.8 %collective-permute-done.6 = bf16[256,1024]{1,0:T(8,128)(2,1)} collective-permute-done((bf16[256,1024]{1,0:T(8,128)(2,1)}, bf16[256,1024]{1,0:T(8,128)(2,1)}, u32[]{:S(2)}, u32[]{:S(2)}) %collective-permute-start.6) | collective-permute-done | bytes 524320 | tf_op jit(solution)/shard_map/ppermute | solution.py:268
  139.7 6.2 %convolution_convert_fusion.1 = bf16[2048,1024]{1,0:T(8,128)(2,1)} fusion(bf16[512,2048]{0,1:T(8,128)(2,1)} %pad_maximum_fusion, bf16[256,1024]{1,0:T(8,128)(2,1)} %collective-permute-done.6, bf16[256,1024]{1,0:T(8,128)(2,1)} %get-tuple-element.55), kind=kOutput, calls=%fused_computation.13 | convolution fusion | flops 2151677952 | bytes 7340032 | tf_op jit(solution)/shard_map/dot_general | solution.py:376
  145.9 10.5 %all-to-all-start.2 = ((f32[64,2,128]{2,1,0:T(2,128)}), f32[64,2,128]{2,1,0:T(2,128)S(1)}, u32[]{:S(2)}, u32[]{:S(2)}) async-start(f32[64,2,128]{2,1,0:T(2,128)} %bitcast.30), calls=%async_computation.2 | async-start | bytes 131072 | tf_op jit(solution)/shard_map/all_to_all | solution.py:253
  156.4 9.6 %mode_sums.1 = (f32[16,8,128]{2,1,0:T(8,128)}, f32[16,8,128]{2,1,0:T(8,128)}, f32[16,8,1024]{2,1,0:T(8,128)}) custom-call(f32[256,1024]{1,0:T(8,128)} %multiply_reduce-precision_fusion.1.refs_0_, f32[256,1024]{1,0:T(8,128)} %get-tuple-element.45.refs_0_.refs_1_, f32[16,1024]{1,0:T(8,128)} %refs_1_.7, f32[16,8,1024]{2,1,0:T(8,128)} %get-tuple-element.42.refs_3_, ...), custom_call_target="tpu_custom_call" | custom-call | flops 33554432 | bytes 2097152 | tf_op jit(solution)/shard_map/mode_sums/pallas_call | solution.py:201
  166.0 2.0 all-to-all-done.2.refs_0_
  170.3 10.8 %all-to-all-start.3 = ((f32[64,2,128]{2,1,0:T(2,128)}), f32[64,2,128]{2,1,0:T(2,128)S(1)}, u32[]{:S(2)}, u32[]{:S(2)}) async-start(f32[64,2,128]{2,1,0:T(2,128)} %slab_scan_back.1), calls=%async_computation.3 | async-start | bytes 131072 | tf_op jit(solution)/shard_map/all_to_all | solution.py:263
  181.2 7.3 %convolution_convert_fusion = bf16[256,4096]{1,0:T(8,128)(2,1)} fusion(bf16[256,1024]{1,0:T(8,128)(2,1)} %get-tuple-element.55, bf16[4096,1024]{1,0:T(8,128)(2,1)} %all-gather.2.cloned.1.call-done), kind=kOutput, calls=%fused_computation.7 | convolution fusion | flops 2148532224 | bytes 11010048 | tf_op jit(solution)/shard_map/dot_general | solution.py:382
  188.5 4.1 %copy.20 = bf16[256,4096]{0,1:T(8,128)(2,1)} copy(bf16[256,4096]{1,0:T(8,128)(2,1)} %convolution_convert_fusion) | data formatting | bytes 4194304 | tf_op jit(solution)/shard_map/convert_element_type | solution.py:383
  192.6 3.2 %copy.21 = bf16[256,2,32,64]{0,3,2,1:T(8,128)(2,1)} copy(bf16[256,2,32,64]{0,3,1,2:T(8,128)(2,1)} %bitcast.120) | data formatting | bytes 4194304 | tf_op jit(solution)/shard_map/transpose | solution.py:287
  196.4 7.6 %modal_backward.1 = (f32[256,1024]{1,0:T(8,128)}, f32[16,8,128]{2,1,0:T(8,128)}) custom-call(f32[256,1024]{1,0:T(8,128)} %get-tuple-element.45.refs_0_.refs_1_, f32[16,1024]{1,0:T(8,128)} %refs_1_.7, f32[16,1024]{1,0:T(8,128)} %get-tuple-element.104.refs_2_, f32[16,8,1024]{2,1,0:T(8,128)} %get-tuple-element.57.refs_3_, f32[16,8,128]{2,1,0:T(8,128)} %bitcast.131, ...), custom_call_target="tpu_custom_call" | custom-call | flops 16777216 | bytes 2097152 | tf_op jit(solution)/shard_map/modal_backward/pallas_call | solution.py:201
  204.0 1.8 fusion.21
  205.9 3.2 %fusion.5 = (f32[3,1024]{1,0:T(4,128)S(1)}, f32[3,1024]{1,0:T(4,128)S(1)}, f32[3,1024]{1,0:T(4,128)S(1)}, f32[3,1024]{1,0:T(4,128)S(1)}, f32[3,1024]{1,0:T(4,128...) fusion(bf16[256,3,1024]{2,0,1:T(8,128)(2,1)S(1)} %copy-done.5, bf16[6,3,1024]{2,0,1:T(8,128)(2,1)S(1)} %collective-permute-done, ...), kind=kLoop, calls=%fused_computation.19 | loop fusion | flops 40872960 | bytes 3268608 | tf_op jit(solution)/shard_map/tjc,tjc->jc/dot_general | solution.py:403
  210.3 12.8 %all-to-all-start.4 = ((f32[64,8,128]{2,1,0:T(8,128)}), f32[64,8,128]{2,1,0:T(8,128)S(1)}, u32[]{:S(2)}, u32[]{:S(2)}) async-start(f32[64,8,128]{2,1,0:T(8,128)} %maximum_maximum_fusion), calls=%async_computation.5 | async-start | bytes 524288 | tf_op jit(solution)/shard_map/all_to_all | solution.py:335
  224.6 2.4 collective-permute-start.7
  227.0 3.7 %collective-permute-done.7 = bf16[6,3,1024]{2,0,1:T(8,128)(2,1)S(1)} collective-permute-done((bf16[6,3,1024]{2,0,1:T(8,128)(2,1)S(1)}, bf16[6,3,1024]{2,0,1:T(8,128)(2,1)S(1)}, u32[]{:S(2)}, u32[]{:S(2)}) %collective-permute-start.7) | collective-permute-done | bytes 36896 | tf_op jit(solution)/shard_map/ppermute | solution.py:303
  232.0 4.5 %all-to-all-done.4 = f32[64,8,128]{2,1,0:T(8,128)S(1)} async-done(((f32[64,8,128]{2,1,0:T(8,128)}), f32[64,8,128]{2,1,0:T(8,128)S(1)}, u32[]{:S(2)}, u32[]{:S(2)}) %all-to-all-start.4) | async-done | bytes 262176 | tf_op jit(solution)/shard_map/all_to_all | solution.py:335
  237.3 8.4 %all-to-all-start.5 = ((f32[64,8,128]{2,1,0:T(8,128)}), f32[64,8,128]{2,1,0:T(8,128)S(1)}, u32[]{:S(2)}, u32[]{:S(2)}) async-start(f32[64,8,128]{2,1,0:T(8,128)} %broadcast_in_dim.14), calls=%async_computation.6 | async-start | bytes 524288 | tf_op jit(solution)/shard_map/all_to_all | solution.py:338
  245.7 1.8 dynamic-slice_bitcast_fusion.2
  247.5 2.7 %collective-permute-start.8 = (bf16[64,1024]{1,0:T(8,128)(2,1)}, bf16[64,1024]{1,0:T(8,128)(2,1)S(1)}, u32[]{:S(2)}, u32[]{:S(2)}) collective-permute-start(bf16[64,1024]{1,0:T(8,128)(2,1)} %get-tuple-element.90), channel_id=1, source_target_pairs={{0,96},{32,0},{64,32},{96,64},{1,97},{33,1},{65,33},{97,65},{2,98}... | collective-permute-start | bytes 393224 | tf_op jit(solution)/shard_map/ppermute | solution.py:268
  250.2 2.3 collective-permute-start.9
  252.5 4.7 %add_convert_fusion = bf16[256,3,1024]{2,0,1:T(8,128)(2,1)} fusion(bf16[262,3,1024]{2,0,1:T(8,128)(2,1)S(1)} %pad_maximum_fusion.1, f32[3,1024]{1,0:T(4,128)S(1)} %get-tuple-element.106, f32[3,1024]{1,0:T(4,128)S(1)} %get-tuple-element.107, f32[3,1024]{1,0:T(4,128)S(1)} %get-tuple-element.108, f32[3,1024]{1,0:T(4,128)S(1)} %get-tuple-element.109, ...), kind=kLoop, calls=%fused_computation.21 | loop fusion | flops 18087936 | bytes 12668928 | tf_op jit(solution)/shard_map/convert_element_type | solution.py:421
  257.2 1.8 all-to-all-done.5
  259.0 2.0 copy.22
  261.1 1.8 fusion.24
  (92 shorter events, 24.2 us)
Async XLA Ops:
  7.2 110.0 %all-gather.2.cloned.1.call-start = ((), (), s32[]{:S(2)}) async-start(), calls=%async_computation.8 | async-start | bytes 8650752 | tf_op jit(solution)/shard_map/all_gather | solution.py:275
  7.2 7.0 %collective-permute-start.4 = (bf16[64,1024]{1,0:T(8,128)(2,1)}, bf16[64,1024]{1,0:T(8,128)(2,1)S(1)}, u32[]{:S(2)}, u32[]{:S(2)}) collective-permute-start(bf16[64,1024]{1,0:T(8,128)(2,1)} %bitcast.135), channel_id=1, source_target_pairs={{0,128},{128,0},{1,129},{129,1},{2,130},{130,2},{3,131},{131,3},{4... | collective-permute-start | bytes 393224 | tf_op jit(solution)/shard_map/ppermute | solution.py:268
  16.7 6.0 %collective-permute-start = (bf16[6,3,1024]{2,0,1:T(8,128)(2,1)S(1)}, bf16[6,3,1024]{2,0,1:T(8,128)(2,1)S(1)}, u32[]{:S(2)}, u32[]{:S(2)}) collective-permute-start(bf16[6,3,1024]{2,0,1:T(8,128)(2,1)S(1)} %slice.96), channel_id=1, source_target_pairs={{0,4},{4,8},{8,12},{12,16},{16,20},{20,24},{24,28},{28,32},{32,36}... | collective-permute-start | bytes 110600 | tf_op jit(solution)/shard_map/ppermute | solution.py:303
  39.4 20.2 %collective-permute-start.1 = (bf16[256,1024]{0,1:T(8,128)(2,1)}, bf16[256,1024]{0,1:T(8,128)(2,1)}, u32[]{:S(2)}, u32[]{:S(2)}) collective-permute-start(bf16[256,1024]{0,1:T(8,128)(2,1)} %copy.13), channel_id=1, source_target_pairs={{0,3},{1,0},{2,1},{3,2},{4,7},{5,4},{6,5},{7,6},{8,11},{9,8},{10,9... | collective-permute-start | bytes 1572872 | tf_op jit(solution)/shard_map/ppermute | solution.py:268
  39.4 26.4 %collective-permute-start.2 = (bf16[256,1024]{0,1:T(8,128)(2,1)}, bf16[256,1024]{0,1:T(8,128)(2,1)}, u32[]{:S(2)}, u32[]{:S(2)}) collective-permute-start(bf16[256,1024]{0,1:T(8,128)(2,1)} %copy.13), channel_id=1, source_target_pairs={{0,2},{1,3},{2,0},{3,1},{4,6},{5,7},{6,4},{7,5},{8,10},{9,11},{10,... | collective-permute-start | bytes 1572872 | tf_op jit(solution)/shard_map/ppermute | solution.py:268
  40.9 26.7 %collective-permute-start.3 = (bf16[256,1024]{0,1:T(8,128)(2,1)}, bf16[256,1024]{0,1:T(8,128)(2,1)}, u32[]{:S(2)}, u32[]{:S(2)}) collective-permute-start(bf16[256,1024]{0,1:T(8,128)(2,1)} %copy.13), channel_id=1, source_target_pairs={{0,1},{1,2},{2,3},{3,0},{4,5},{5,6},{6,7},{7,4},{8,9},{9,10},{10,1... | collective-permute-start | bytes 1572872 | tf_op jit(solution)/shard_map/ppermute | solution.py:268
  41.1 28.4 %all-to-all-start = ((f32[64,2,128]{2,1,0:T(2,128)}), f32[64,2,128]{2,1,0:T(2,128)S(1)}, u32[]{:S(2)}, u32[]{:S(2)}) async-start(f32[64,2,128]{2,1,0:T(2,128)} %bitcast.136), calls=%async_computation | async-start | bytes 131072 | tf_op jit(solution)/shard_map/all_to_all | solution.py:253
  69.5 6.7 %copy-start.6 = (f32[16,1024]{1,0:T(8,128)S(1)}, f32[16,1024]{1,0:T(8,128)}, u32[]{:S(2)}) copy-start(f32[16,1024]{1,0:T(8,128)} %refs_1_.7) | copy-start | bytes 196612
  69.5 6.7 %copy-start.13 = (f32[16,1024]{1,0:T(8,128)S(1)}, f32[16,1024]{1,0:T(8,128)}, u32[]{:S(2)}) copy-start(f32[16,1024]{1,0:T(8,128)} %param.8) | copy-start | bytes 196612
  69.6 4.0 %copy-start.11 = (f32[64,2,128]{2,1,0:T(2,128)}, f32[64,2,128]{2,1,0:T(2,128)S(1)}, u32[]{:S(2)}) copy-start(f32[64,2,128]{2,1,0:T(2,128)S(1)} %all-to-all-done.refs_0_) | copy-start | bytes 196612
  73.5 40.7 %collective-permute-start.5 = (bf16[256,2048]{0,1:T(8,128)(2,1)}, bf16[256,2048]{0,1:T(8,128)(2,1)}, u32[]{:S(2)}, u32[]{:S(2)}) collective-permute-start(bf16[256,2048]{0,1:T(8,128)(2,1)} %bitcast.29), channel_id=1, source_target_pairs={{0,128},{128,0},{1,129},{129,1},{2,130},{130,2},{3,131},{131,3},{4... | collective-permute-start | bytes 3145736 | tf_op jit(solution)/shard_map/ppermute | solution.py:268
  79.2 24.9 %all-to-all-start.1 = ((f32[64,2,128]{2,1,0:T(2,128)}), f32[64,2,128]{2,1,0:T(2,128)S(1)}, u32[]{:S(2)}, u32[]{:S(2)}) async-start(f32[64,2,128]{2,1,0:T(2,128)} %slab_scan.1), calls=%async_computation.1 | async-start | bytes 131072 | tf_op jit(solution)/shard_map/all_to_all | solution.py:263
  92.3 153.4 %reduce-scatter.5.cloned.1.call-start = ((), (), s32[]{:S(2)}) async-start(), calls=%async_computation.10 | async-start | bytes 4718592 | tf_op jit(solution)/shard_map/reduce_scatter | solution.py:319
  104.2 0.6 copy-start.9
  117.2 6.4 %copy-start.8 = (bf16[256,1024]{1,0:T(8,128)(2,1)S(1)}, bf16[256,1024]{1,0:T(8,128)(2,1)}, u32[]{:S(2)}) copy-start(bf16[256,1024]{1,0:T(8,128)(2,1)} %convert_element_type.99) | copy-start | bytes 1572868
  125.1 14.6 %collective-permute-start.6 = (bf16[256,1024]{1,0:T(8,128)(2,1)}, bf16[256,1024]{1,0:T(8,128)(2,1)}, u32[]{:S(2)}, u32[]{:S(2)}) collective-permute-start(bf16[256,1024]{1,0:T(8,128)(2,1)} %get-tuple-element.55), channel_id=1, source_target_pairs={{0,128},{128,0},{1,129},{129,1},{2,130},{130,2},{3,131},{131,3},{4... | collective-permute-start | bytes 1572872 | tf_op jit(solution)/shard_map/ppermute | solution.py:268
  145.9 22.1 %all-to-all-start.2 = ((f32[64,2,128]{2,1,0:T(2,128)}), f32[64,2,128]{2,1,0:T(2,128)S(1)}, u32[]{:S(2)}, u32[]{:S(2)}) async-start(f32[64,2,128]{2,1,0:T(2,128)} %bitcast.30), calls=%async_computation.2 | async-start | bytes 131072 | tf_op jit(solution)/shard_map/all_to_all | solution.py:253
  168.0 0.6 copy-start.12
  170.3 25.5 %all-to-all-start.3 = ((f32[64,2,128]{2,1,0:T(2,128)}), f32[64,2,128]{2,1,0:T(2,128)S(1)}, u32[]{:S(2)}, u32[]{:S(2)}) async-start(f32[64,2,128]{2,1,0:T(2,128)} %slab_scan_back.1), calls=%async_computation.3 | async-start | bytes 131072 | tf_op jit(solution)/shard_map/all_to_all | solution.py:263
  181.1 77.9 %reduce-scatter.3.cloned.1.call-start = ((), (), s32[]{:S(2)}) async-start(), calls=%async_computation.9 | async-start | bytes 2621440 | tf_op jit(solution)/shard_map/reduce_scatter | solution.py:389
  195.8 0.6 copy-start.10
  204.0 1.8 copy-start
  204.0 1.9 copy-start.5
  204.0 5.5 %copy-start.14 = (f32[16,8,128]{2,1,0:T(8,128)S(1)}, f32[16,8,128]{2,1,0:T(8,128)}, u32[]{:S(2)}) copy-start(f32[16,8,128]{2,1,0:T(8,128)} %get-tuple-element.62) | copy-start | bytes 196612
  204.0 5.5 %copy-start.15 = (f32[16,8,128]{2,1,0:T(8,128)S(1)}, f32[16,8,128]{2,1,0:T(8,128)}, u32[]{:S(2)}) copy-start(f32[16,8,128]{2,1,0:T(8,128)} %get-tuple-element.63) | copy-start | bytes 196612
  205.8 3.3 %copy-start.2 = (bf16[256,1,1024]{2,0,1:T(8,128)(2,1)}, bf16[256,1,1024]{2,0,1:T(8,128)(2,1)S(1)}, u32[]{:S(2)}) copy-start(bf16[256,1,1024]{2,0,1:T(8,128)(2,1)S(1)} %get-tuple-element.79) | copy-start | bytes 1572868
  205.8 3.3 %copy-start.4 = (bf16[256,1,1024]{2,0,1:T(8,128)(2,1)}, bf16[256,1,1024]{2,0,1:T(8,128)(2,1)S(1)}, u32[]{:S(2)}) copy-start(bf16[256,1,1024]{2,0,1:T(8,128)(2,1)S(1)} %get-tuple-element.80) | copy-start | bytes 1572868
  205.8 17.4 %copy-start.1 = (bf16[256,1,1024]{2,0,1:T(8,128)(2,1)S(1)}, bf16[256,1,1024]{2,0,1:T(8,128)(2,1)}, u32[]{:S(2)}) copy-start(bf16[256,1,1024]{2,0,1:T(8,128)(2,1)} %get-tuple-element.89) | copy-start | bytes 1572868
  209.2 21.6 %copy-start.3 = (bf16[256,1,1024]{2,0,1:T(8,128)(2,1)S(1)}, bf16[256,1,1024]{2,0,1:T(8,128)(2,1)}, u32[]{:S(2)}) copy-start(bf16[256,1,1024]{2,0,1:T(8,128)(2,1)} %copy-done.2) | copy-start | bytes 1572868
  210.3 26.2 %all-to-all-start.4 = ((f32[64,8,128]{2,1,0:T(8,128)}), f32[64,8,128]{2,1,0:T(8,128)S(1)}, u32[]{:S(2)}, u32[]{:S(2)}) async-start(f32[64,8,128]{2,1,0:T(8,128)} %maximum_maximum_fusion), calls=%async_computation.5 | async-start | bytes 524288 | tf_op jit(solution)/shard_map/all_to_all | solution.py:335
  224.6 6.2 %collective-permute-start.7 = (bf16[6,3,1024]{2,0,1:T(8,128)(2,1)S(1)}, bf16[6,3,1024]{2,0,1:T(8,128)(2,1)S(1)}, u32[]{:S(2)}, u32[]{:S(2)}) collective-permute-start(bf16[6,3,1024]{2,0,1:T(8,128)(2,1)S(1)} %slice.134), channel_id=1, source_target_pairs={{4,0},{8,4},{12,8},{16,12},{20,16},{24,20},{28,24},{32,28},{36,32}... | collective-permute-start | bytes 110600 | tf_op jit(solution)/shard_map/ppermute | solution.py:303
  237.3 21.7 %all-to-all-start.5 = ((f32[64,8,128]{2,1,0:T(8,128)}), f32[64,8,128]{2,1,0:T(8,128)S(1)}, u32[]{:S(2)}, u32[]{:S(2)}) async-start(f32[64,8,128]{2,1,0:T(8,128)} %broadcast_in_dim.14), calls=%async_computation.6 | async-start | bytes 524288 | tf_op jit(solution)/shard_map/all_to_all | solution.py:338
  247.5 13.6 %collective-permute-start.8 = (bf16[64,1024]{1,0:T(8,128)(2,1)}, bf16[64,1024]{1,0:T(8,128)(2,1)S(1)}, u32[]{:S(2)}, u32[]{:S(2)}) collective-permute-start(bf16[64,1024]{1,0:T(8,128)(2,1)} %get-tuple-element.90), channel_id=1, source_target_pairs={{0,96},{32,0},{64,32},{96,64},{1,97},{33,1},{65,33},{97,65},{2,98}... | collective-permute-start | bytes 393224 | tf_op jit(solution)/shard_map/ppermute | solution.py:268
  250.2 10.9 %collective-permute-start.10 = (bf16[64,1024]{1,0:T(8,128)(2,1)}, bf16[64,1024]{1,0:T(8,128)(2,1)}, u32[]{:S(2)}, u32[]{:S(2)}) collective-permute-start(bf16[64,1024]{1,0:T(8,128)(2,1)} %get-tuple-element.91), channel_id=1, source_target_pairs={{0,32},{32,64},{64,96},{96,0},{1,33},{33,65},{65,97},{97,1},{2,34}... | collective-permute-start | bytes 393224 | tf_op jit(solution)/shard_map/ppermute | solution.py:268
  250.2 12.7 %copy-start.7 = (f32[16,1024]{1,0:T(8,128)S(1)}, f32[16,1024]{1,0:T(8,128)}, u32[]{:S(2)}) copy-start(f32[16,1024]{1,0:T(8,128)} %refs_1_.7) | copy-start | bytes 196612
  250.2 10.8 %collective-permute-start.9 = (bf16[64,1024]{1,0:T(8,128)(2,1)S(1)}, bf16[64,1024]{1,0:T(8,128)(2,1)}, u32[]{:S(2)}, u32[]{:S(2)}) collective-permute-start(bf16[64,1024]{1,0:T(8,128)(2,1)S(1)} %get-tuple-element.92), channel_id=1, source_target_pairs={{0,64},{32,96},{64,0},{96,32},{1,65},{33,97},{65,1},{97,33},{2,66}... | collective-permute-start | bytes 393224 | tf_op jit(solution)/shard_map/ppermute | solution.py:268
Sparse Core Ops, SparseCore 0:
  16.0 100.7 all-gather.1
  146.1 54.6 reduce-scatter.4
  203.3 33.7 reduce-scatter.2

commit v3 on v2

--- a/solution.py
+++ b/solution.py
@@ -380,13 +380,12 @@
     adj_outer, (_, sums_here, gated) = entering(adj_ends, slab_decay, True, beside)
     alpha_rows, beta_part, slopes = sums_here
     partial_out = lax.dot_general(gated, weight, (((1,), (1,)), ((), ())), preferred_element_type=F32)
-    partial_out = from_gather_order(partial_out.astype(BF16))
-    adj_outer, partial_out = lax.optimization_barrier((adj_outer, partial_out))
+    adj_outer, partial_out = lax.optimization_barrier((adj_outer, partial_out.astype(BF16)))
     grad_product, beta_rows = backward_output(
         grad_conv, decay_rate, coeffs, adj_enter, adj_outer, slopes, beta_part
     )
     grad_product = grad_product.astype(BF16)
-    mixed = lax.psum_scatter(partial_out, "tp", scatter_dimension=1, tiled=True)
+    mixed = lax.psum_scatter(from_gather_order(partial_out), "tp", scatter_dimension=1, tiled=True)
 
     grad_query = (grad_gated * convolved).astype(BF16)
     grad_key = (grad_product * valued).astype(BF16)

time: 273 us -> 273 us (level)
  waiting for transfers between devices: 32.8 us -> 37.5 us
  starting transfers between devices: 92.3 us -> 87.7 us
    all_to_all x2, waiting for transfers between devices: 6.26 us -> 10.9 us  [entering(): outer = lax.all_to_all(scanned, SEQ, 0, 0, tiled=True).reshape(ends.shape)]
    all_to_all x1, starting transfers between devices: 12.8 us -> 8.18 us  [total_over_slabs(): pieces = lax.all_to_all(rows.reshape(shape), SEQ, 0, 0, tiled=True)]
    optimization_barrier x0 -> x1, local copies, waits for them, and re-layouts: none -> 4.1 us  [local(): lax.optimization_barrier((adj_outer, partial_out.astype(BF16)))]
    convert_element_type x1 -> x0, local copies, waits for them, and re-layouts: 4.06 us -> none  [local(): partial_out = from_gather_order(partial_out.astype(BF16))]
  transfers between devices with their start and end apart: 20 -> 20, of which waited for: 9 -> 10; matrix products, arithmetic and copies ran while one was open for 26% -> 26% of each run, Pallas kernels for 15% -> 15%
where the time goes in v3:
time: 273 us; the launch traced here: 270 us
  starting transfers between devices  87.7 us (32%)
  Pallas kernels  40 us (15%)
  local copies, waits for them, and re-layouts  37.9 us (14%)
  waiting for transfers between devices  37.5 us (14%)
  other arithmetic  33.1 us (12%)
  matrix products  19.9 us (7%)
  between operations  14.2 us (5%)
    pallas_call x5, Pallas kernels, modal_call(): pl.pallas_call(lane_groups(body), name=name, grid=(channels // block,), i...  36.8 us
    all_to_all x2, starting transfers between devices, entering(): gathered = lax.all_to_all(ends.reshape(shape), SEQ, 0, 0, tiled=True)  25.6 us
    all_to_all x2, starting transfers between devices, entering(): outer = lax.all_to_all(scanned, SEQ, 0, 0, tiled=True).reshape(ends.shape)  23.9 us
    ppermute x9, starting transfers between devices, ring(): lax.ppermute(array, axis, [(i, (i + by) % size) for i in range(size)])  15.2 us
    ppermute x9, waiting for transfers between devices, ring(): lax.ppermute(array, axis, [(i, (i + by) % size) for i in range(size)])  13.9 us
    all_to_all x2, waiting for transfers between devices, entering(): outer = lax.all_to_all(scanned, SEQ, 0, 0, tiled=True).reshape(ends.shape)  10.9 us
    all_to_all x1, starting transfers between devices, total_over_slabs(): lax.all_to_all(copies, SEQ, 0, 0, tiled=True).reshape(count, channels)  8.45 us
    all_to_all x1, starting transfers between devices, total_over_slabs(): pieces = lax.all_to_all(rows.reshape(shape), SEQ, 0, 0, tiled=True)  8.18 us
  transfers between devices with their start and end apart: 20, of which 10 were waited for; matrix products, arithmetic and copies ran while one was open for 26% of the time, Pallas kernels for 15%

profile of v3, /device:TPU:32, one launch (start us, length us, event | category | flops | bytes accessed | tf_op | source)
XLA Modules:
  0.0 270.3 jit_solution(16795545067443672570)
XLA Ops:
  7.2 3.1 %collective-permute-start.4 = (bf16[64,1024]{1,0:T(8,128)(2,1)}, bf16[64,1024]{1,0:T(8,128)(2,1)S(1)}, u32[]{:S(2)}, u32[]{:S(2)}) collective-permute-start(bf16[64,1024]{1,0:T(8,128)(2,1)} %bitcast.135), channel_id=1, source_target_pairs={{0,128},{128,0},{1,129},{129,1},{2,130},{130,2},{3,131},{131,3},{4... | collective-permute-start | bytes 393224 | tf_op jit(solution)/shard_map/ppermute | solution.py:268
  10.3 3.9 %collective-permute-done.4 = bf16[64,1024]{1,0:T(8,128)(2,1)S(1)} collective-permute-done((bf16[64,1024]{1,0:T(8,128)(2,1)}, bf16[64,1024]{1,0:T(8,128)(2,1)S(1)}, u32[]{:S(2)}, u32[]{:S(2)}) %collective-permute-start.4) | collective-permute-done | bytes 131104 | tf_op jit(solution)/shard_map/ppermute | solution.py:268
  16.7 3.8 %collective-permute-start = (bf16[6,3,1024]{2,0,1:T(8,128)(2,1)S(1)}, bf16[6,3,1024]{2,0,1:T(8,128)(2,1)S(1)}, u32[]{:S(2)}, u32[]{:S(2)}) collective-permute-start(bf16[6,3,1024]{2,0,1:T(8,128)(2,1)S(1)} %slice.96), channel_id=1, source_target_pairs={{0,4},{4,8},{8,12},{12,16},{16,20},{20,24},{24,28},{28,32},{32,36}... | collective-permute-start | bytes 110600 | tf_op jit(solution)/shard_map/ppermute | solution.py:303
  22.7 7.2 %multiply_add_fusion = f32[256,3,1024]{2,0,1:T(8,128)S(1)} fusion(bf16[256,3,1024]{2,0,1:T(8,128)(2,1)} %param.6, bf16[6,3,1024]{2,0,1:T(8,128)(2,1)S(1)} %collective-permute-done, f32[3,1024]{1,0:T(4,128)S(1)} %get-tuple-element.106, f32[3,1024]{1,0:T(4,128)S(1)} %get-tuple-element.107, f32[3,1024]{1,0:T(4,128)S(1)} %get-tuple-element.108, ...), kind=kLoop, calls=%fused_computation.22 | loop fusion | flops 29884416 | bytes 4841472 | tf_op jit(solution)/shard_map/add | solution.py:353
  31.2 6.2 %state_ends.1 = (f32[16,8,128]{2,1,0:T(8,128)}, f32[16,8,1024]{2,1,0:T(8,128)}) custom-call(f32[256,1024]{1,0:T(8,128)} %multiply_reduce-precision_fusion.1.refs_0_, f32[16,1024]{1,0:T(8,128)} %refs_1_.7), custom_call_target="tpu_custom_call" | custom-call | flops 8388608 | bytes 2097152 | tf_op jit(solution)/shard_map/state_ends/pallas_call | solution.py:201
  37.3 2.1 copy.13
  41.1 15.1 %all-to-all-start = ((f32[64,2,128]{2,1,0:T(2,128)}), f32[64,2,128]{2,1,0:T(2,128)S(1)}, u32[]{:S(2)}, u32[]{:S(2)}) async-start(f32[64,2,128]{2,1,0:T(2,128)} %bitcast.136), calls=%async_computation | async-start | bytes 131072 | tf_op jit(solution)/shard_map/all_to_all | solution.py:253
  57.8 1.9 constant_dynamic-update-slice_fusion.3
  59.7 1.9 constant_dynamic-update-slice_fusion.2
  61.5 4.2 %collective-permute-done.2 = bf16[256,1024]{0,1:T(8,128)(2,1)} collective-permute-done((bf16[256,1024]{0,1:T(8,128)(2,1)}, bf16[256,1024]{0,1:T(8,128)(2,1)}, u32[]{:S(2)}, u32[]{:S(2)}) %collective-permute-start.2) | collective-permute-done | bytes 524320 | tf_op jit(solution)/shard_map/ppermute | solution.py:268
  65.8 1.9 constant_dynamic-update-slice_fusion.1
  67.7 1.9 constant_dynamic-update-slice_fusion
  69.6 2.9 %constant_dynamic-slice_fusion.1 = (bf16[256,2048]{0,1:T(8,128)(2,1)}, bf16[256,2048]{0,1:T(8,128)(2,1)S(1)}) fusion(bf16[256,4096]{0,1:T(8,128)(2,1)} %constant_dynamic-update-slice_fusion, s32[]{:T(128)S(6)} %select_n.95, s32[]{:T(128)S(6)} %select_n.96), kind=kLoop, calls=%fused_computation.77 | loop fusion | bytes 4194312 | tf_op jit(solution)/shard_map/dynamic_slice | solution.py:312
  73.5 2.7 %collective-permute-start.5 = (bf16[256,2048]{0,1:T(8,128)(2,1)}, bf16[256,2048]{0,1:T(8,128)(2,1)}, u32[]{:S(2)}, u32[]{:S(2)}) collective-permute-start(bf16[256,2048]{0,1:T(8,128)(2,1)} %bitcast.29), channel_id=1, source_target_pairs={{0,128},{128,0},{1,129},{129,1},{2,130},{130,2},{3,131},{131,3},{4... | collective-permute-start | bytes 3145736 | tf_op jit(solution)/shard_map/ppermute | solution.py:268
  79.2 13.1 %all-to-all-start.1 = ((f32[64,2,128]{2,1,0:T(2,128)}), f32[64,2,128]{2,1,0:T(2,128)S(1)}, u32[]{:S(2)}, u32[]{:S(2)}) async-start(f32[64,2,128]{2,1,0:T(2,128)} %slab_scan.1), calls=%async_computation.1 | async-start | bytes 131072 | tf_op jit(solution)/shard_map/all_to_all | solution.py:263
  92.4 2.3 copy.18
  94.7 3.2 %copy.17 = bf16[256,32,2,64]{0,3,2,1:T(8,128)(2,1)} copy(bf16[256,32,2,64]{0,3,1,2:T(8,128)(2,1)} %bitcast.20) | data formatting | bytes 4194304 | tf_op jit(solution)/shard_map/transpose | solution.py:281
  97.9 6.3 %all-to-all-done.1 = f32[64,2,128]{2,1,0:T(2,128)S(1)} async-done(((f32[64,2,128]{2,1,0:T(2,128)}), f32[64,2,128]{2,1,0:T(2,128)S(1)}, u32[]{:S(2)}, u32[]{:S(2)}) %all-to-all-start.1) | async-done | bytes 65568 | tf_op jit(solution)/shard_map/all_to_all | solution.py:263
  104.8 7.3 %modal_forward.1 = f32[256,1024]{1,0:T(8,128)} custom-call(f32[256,1024]{1,0:T(8,128)} %multiply_reduce-precision_fusion.1.refs_0_, f32[16,1024]{1,0:T(8,128)} %refs_1_.7, f32[16,1024]{1,0:T(8,128)} %get-tuple-element.104.refs_2_, f32[16,8,1024]{2,1,0:T(8,128)} %get-tuple-element.42.refs_3_, f32[16,8,128]{2,1,0:T(8,128)} %bitcast.127), custom_call_target="tpu_custom_call" | custom-call | flops 16777216 | bytes 2097152 | tf_op jit(solution)/shard_map/modal_forward/pallas_call | solution.py:201
  112.1 2.1 convert_element_type.99
  114.2 3.0 %pad_maximum_fusion = bf16[512,2048]{0,1:T(8,128)(2,1)} fusion(bf16[256,2048]{0,1:T(8,128)(2,1)} %collective-permute-done.5, bf16[256,2048]{0,1:T(8,128)(2,1)} %bitcast.123), kind=kLoop, calls=%fused_computation.23 | loop fusion | flops 4194304 | bytes 4194304 | tf_op jit(solution)/shard_map/concatenate | solution.py:315
  117.2 6.4 %convolution_reduce-precision_fusion = f32[256,1024]{1,0:T(8,128)S(1)} fusion(bf16[256,4096]{0,1:T(8,128)(2,1)} %bitcast.118, bf16[4096,1024]{1,0:T(8,128)(2,1)} %all-gather.2.cloned.1.call-done), kind=kOutput, calls=%fused_computation.33 | convolution fusion | flops 2147745792 | bytes 11534336 | tf_op jit(solution)/shard_map/dot_general | solution.py:369
  125.1 2.6 collective-permute-start.6
  127.8 6.2 %adjoint_ends.1 = (f32[16,8,128]{2,1,0:T(8,128)}, f32[16,8,1024]{2,1,0:T(8,128)}) custom-call(f32[256,1024]{1,0:T(8,128)} %get-tuple-element.45.refs_0_.refs_1_, f32[16,1024]{1,0:T(8,128)} %refs_1_.7), custom_call_target="tpu_custom_call" | custom-call | flops 8388608 | bytes 2097152 | tf_op jit(solution)/shard_map/adjoint_ends/pallas_call | solution.py:201
  134.0 5.8 %collective-permute-done.6 = bf16[256,1024]{1,0:T(8,128)(2,1)} collective-permute-done((bf16[256,1024]{1,0:T(8,128)(2,1)}, bf16[256,1024]{1,0:T(8,128)(2,1)}, u32[]{:S(2)}, u32[]{:S(2)}) %collective-permute-start.6) | collective-permute-done | bytes 524320 | tf_op jit(solution)/shard_map/ppermute | solution.py:268
  139.7 6.2 %convolution_convert_fusion.1 = bf16[2048,1024]{1,0:T(8,128)(2,1)} fusion(bf16[512,2048]{0,1:T(8,128)(2,1)} %pad_maximum_fusion, bf16[256,1024]{1,0:T(8,128)(2,1)} %collective-permute-done.6, bf16[256,1024]{1,0:T(8,128)(2,1)} %get-tuple-element.55), kind=kOutput, calls=%fused_computation.13 | convolution fusion | flops 2151677952 | bytes 7340032 | tf_op jit(solution)/shard_map/dot_general | solution.py:376
  145.9 10.5 %all-to-all-start.2 = ((f32[64,2,128]{2,1,0:T(2,128)}), f32[64,2,128]{2,1,0:T(2,128)S(1)}, u32[]{:S(2)}, u32[]{:S(2)}) async-start(f32[64,2,128]{2,1,0:T(2,128)} %bitcast.30), calls=%async_computation.2 | async-start | bytes 131072 | tf_op jit(solution)/shard_map/all_to_all | solution.py:253
  156.4 9.6 %mode_sums.1 = (f32[16,8,128]{2,1,0:T(8,128)}, f32[16,8,128]{2,1,0:T(8,128)}, f32[16,8,1024]{2,1,0:T(8,128)}) custom-call(f32[256,1024]{1,0:T(8,128)} %multiply_reduce-precision_fusion.1.refs_0_, f32[256,1024]{1,0:T(8,128)} %get-tuple-element.45.refs_0_.refs_1_, f32[16,1024]{1,0:T(8,128)} %refs_1_.7, f32[16,8,1024]{2,1,0:T(8,128)} %get-tuple-element.42.refs_3_, ...), custom_call_target="tpu_custom_call" | custom-call | flops 33554432 | bytes 2097152 | tf_op jit(solution)/shard_map/mode_sums/pallas_call | solution.py:201
  166.0 2.0 all-to-all-done.2.refs_0_
  170.3 10.8 %all-to-all-start.3 = ((f32[64,2,128]{2,1,0:T(2,128)}), f32[64,2,128]{2,1,0:T(2,128)S(1)}, u32[]{:S(2)}, u32[]{:S(2)}) async-start(f32[64,2,128]{2,1,0:T(2,128)} %slab_scan_back.1), calls=%async_computation.3 | async-start | bytes 131072 | tf_op jit(solution)/shard_map/all_to_all | solution.py:263
  181.2 7.3 %convolution_convert_fusion = bf16[256,4096]{1,0:T(8,128)(2,1)} fusion(bf16[256,1024]{1,0:T(8,128)(2,1)} %get-tuple-element.55, bf16[4096,1024]{1,0:T(8,128)(2,1)} %all-gather.2.cloned.1.call-done), kind=kOutput, calls=%fused_computation.7 | convolution fusion | flops 2148532224 | bytes 11010048 | tf_op jit(solution)/shard_map/dot_general | solution.py:382
  188.5 4.7 %all-to-all-done.3 = f32[64,2,128]{2,1,0:T(2,128)S(1)} async-done(((f32[64,2,128]{2,1,0:T(2,128)}), f32[64,2,128]{2,1,0:T(2,128)S(1)}, u32[]{:S(2)}, u32[]{:S(2)}) %all-to-all-start.3) | async-done | bytes 65568 | tf_op jit(solution)/shard_map/all_to_all | solution.py:263
  193.2 4.1 %copy.20 = bf16[256,4096]{0,1:T(8,128)(2,1)} copy(bf16[256,4096]{1,0:T(8,128)(2,1)} %convolution_convert_fusion) | data formatting | bytes 4194304 | tf_op jit(solution)/shard_map/optimization_barrier | solution.py:383
  197.2 3.2 %copy.21 = bf16[256,2,32,64]{0,3,2,1:T(8,128)(2,1)} copy(bf16[256,2,32,64]{0,3,1,2:T(8,128)(2,1)} %bitcast.120) | data formatting | bytes 4194304 | tf_op jit(solution)/shard_map/transpose | solution.py:287
  200.6 7.6 %modal_backward.1 = (f32[256,1024]{1,0:T(8,128)}, f32[16,8,128]{2,1,0:T(8,128)}) custom-call(f32[256,1024]{1,0:T(8,128)} %get-tuple-element.45.refs_0_.refs_1_, f32[16,1024]{1,0:T(8,128)} %refs_1_.7, f32[16,1024]{1,0:T(8,128)} %get-tuple-element.104.refs_2_, f32[16,8,1024]{2,1,0:T(8,128)} %get-tuple-element.57.refs_3_, f32[16,8,128]{2,1,0:T(8,128)} %bitcast.131, ...), custom_call_target="tpu_custom_call" | custom-call | flops 16777216 | bytes 2097152 | tf_op jit(solution)/shard_map/modal_backward/pallas_call | solution.py:201
  210.1 3.2 %fusion.5 = (f32[3,1024]{1,0:T(4,128)S(1)}, f32[3,1024]{1,0:T(4,128)S(1)}, f32[3,1024]{1,0:T(4,128)S(1)}, f32[3,1024]{1,0:T(4,128)S(1)}, f32[3,1024]{1,0:T(4,128...) fusion(bf16[256,3,1024]{2,0,1:T(8,128)(2,1)S(1)} %copy-done.5, bf16[6,3,1024]{2,0,1:T(8,128)(2,1)S(1)} %collective-permute-done, ...), kind=kLoop, calls=%fused_computation.19 | loop fusion | flops 40872960 | bytes 3268608 | tf_op jit(solution)/shard_map/tjc,tjc->jc/dot_general | solution.py:402
  214.5 8.2 %all-to-all-start.4 = ((f32[64,8,128]{2,1,0:T(8,128)}), f32[64,8,128]{2,1,0:T(8,128)S(1)}, u32[]{:S(2)}, u32[]{:S(2)}) async-start(f32[64,8,128]{2,1,0:T(8,128)} %maximum_maximum_fusion), calls=%async_computation.5 | async-start | bytes 524288 | tf_op jit(solution)/shard_map/all_to_all | solution.py:335
  224.1 2.4 collective-permute-start.7
  226.6 3.7 %collective-permute-done.7 = bf16[6,3,1024]{2,0,1:T(8,128)(2,1)S(1)} collective-permute-done((bf16[6,3,1024]{2,0,1:T(8,128)(2,1)S(1)}, bf16[6,3,1024]{2,0,1:T(8,128)(2,1)S(1)}, u32[]{:S(2)}, u32[]{:S(2)}) %collective-permute-start.7) | collective-permute-done | bytes 36896 | tf_op jit(solution)/shard_map/ppermute | solution.py:303
  231.5 4.5 %all-to-all-done.4 = f32[64,8,128]{2,1,0:T(8,128)S(1)} async-done(((f32[64,8,128]{2,1,0:T(8,128)}), f32[64,8,128]{2,1,0:T(8,128)S(1)}, u32[]{:S(2)}, u32[]{:S(2)}) %all-to-all-start.4) | async-done | bytes 262176 | tf_op jit(solution)/shard_map/all_to_all | solution.py:335
  236.8 8.4 %all-to-all-start.5 = ((f32[64,8,128]{2,1,0:T(8,128)}), f32[64,8,128]{2,1,0:T(8,128)S(1)}, u32[]{:S(2)}, u32[]{:S(2)}) async-start(f32[64,8,128]{2,1,0:T(8,128)} %broadcast_in_dim.14), calls=%async_computation.6 | async-start | bytes 524288 | tf_op jit(solution)/shard_map/all_to_all | solution.py:338
  245.3 1.8 dynamic-slice_bitcast_fusion.2
  247.0 2.7 %collective-permute-start.8 = (bf16[64,1024]{1,0:T(8,128)(2,1)}, bf16[64,1024]{1,0:T(8,128)(2,1)S(1)}, u32[]{:S(2)}, u32[]{:S(2)}) collective-permute-start(bf16[64,1024]{1,0:T(8,128)(2,1)} %get-tuple-element.90), channel_id=1, source_target_pairs={{0,96},{32,0},{64,32},{96,64},{1,97},{33,1},{65,33},{97,65},{2,98}... | collective-permute-start | bytes 393224 | tf_op jit(solution)/shard_map/ppermute | solution.py:268
  249.8 2.3 collective-permute-start.9
  252.0 4.7 %add_convert_fusion = bf16[256,3,1024]{2,0,1:T(8,128)(2,1)} fusion(bf16[262,3,1024]{2,0,1:T(8,128)(2,1)S(1)} %pad_maximum_fusion.1, f32[3,1024]{1,0:T(4,128)S(1)} %get-tuple-element.106, f32[3,1024]{1,0:T(4,128)S(1)} %get-tuple-element.107, f32[3,1024]{1,0:T(4,128)S(1)} %get-tuple-element.108, f32[3,1024]{1,0:T(4,128)S(1)} %get-tuple-element.109, ...), kind=kLoop, calls=%fused_computation.21 | loop fusion | flops 18087936 | bytes 12668928 | tf_op jit(solution)/shard_map/convert_element_type | solution.py:420
  256.7 1.8 all-to-all-done.5
  258.6 2.0 copy.22
  260.6 1.8 fusion.24
  (92 shorter events, 25.4 us)
Async XLA Ops:
  7.2 110.0 %all-gather.2.cloned.1.call-start = ((), (), s32[]{:S(2)}) async-start(), calls=%async_computation.8 | async-start | bytes 8650752 | tf_op jit(solution)/shard_map/all_gather | solution.py:275
  7.2 7.0 %collective-permute-start.4 = (bf16[64,1024]{1,0:T(8,128)(2,1)}, bf16[64,1024]{1,0:T(8,128)(2,1)S(1)}, u32[]{:S(2)}, u32[]{:S(2)}) collective-permute-start(bf16[64,1024]{1,0:T(8,128)(2,1)} %bitcast.135), channel_id=1, source_target_pairs={{0,128},{128,0},{1,129},{129,1},{2,130},{130,2},{3,131},{131,3},{4... | collective-permute-start | bytes 393224 | tf_op jit(solution)/shard_map/ppermute | solution.py:268
  16.7 6.0 %collective-permute-start = (bf16[6,3,1024]{2,0,1:T(8,128)(2,1)S(1)}, bf16[6,3,1024]{2,0,1:T(8,128)(2,1)S(1)}, u32[]{:S(2)}, u32[]{:S(2)}) collective-permute-start(bf16[6,3,1024]{2,0,1:T(8,128)(2,1)S(1)} %slice.96), channel_id=1, source_target_pairs={{0,4},{4,8},{8,12},{12,16},{16,20},{20,24},{24,28},{28,32},{32,36}... | collective-permute-start | bytes 110600 | tf_op jit(solution)/shard_map/ppermute | solution.py:303
  39.4 20.2 %collective-permute-start.1 = (bf16[256,1024]{0,1:T(8,128)(2,1)}, bf16[256,1024]{0,1:T(8,128)(2,1)}, u32[]{:S(2)}, u32[]{:S(2)}) collective-permute-start(bf16[256,1024]{0,1:T(8,128)(2,1)} %copy.13), channel_id=1, source_target_pairs={{0,3},{1,0},{2,1},{3,2},{4,7},{5,4},{6,5},{7,6},{8,11},{9,8},{10,9... | collective-permute-start | bytes 1572872 | tf_op jit(solution)/shard_map/ppermute | solution.py:268
  39.4 26.4 %collective-permute-start.2 = (bf16[256,1024]{0,1:T(8,128)(2,1)}, bf16[256,1024]{0,1:T(8,128)(2,1)}, u32[]{:S(2)}, u32[]{:S(2)}) collective-permute-start(bf16[256,1024]{0,1:T(8,128)(2,1)} %copy.13), channel_id=1, source_target_pairs={{0,2},{1,3},{2,0},{3,1},{4,6},{5,7},{6,4},{7,5},{8,10},{9,11},{10,... | collective-permute-start | bytes 1572872 | tf_op jit(solution)/shard_map/ppermute | solution.py:268
  40.9 26.7 %collective-permute-start.3 = (bf16[256,1024]{0,1:T(8,128)(2,1)}, bf16[256,1024]{0,1:T(8,128)(2,1)}, u32[]{:S(2)}, u32[]{:S(2)}) collective-permute-start(bf16[256,1024]{0,1:T(8,128)(2,1)} %copy.13), channel_id=1, source_target_pairs={{0,1},{1,2},{2,3},{3,0},{4,5},{5,6},{6,7},{7,4},{8,9},{9,10},{10,1... | collective-permute-start | bytes 1572872 | tf_op jit(solution)/shard_map/ppermute | solution.py:268
  41.1 28.4 %all-to-all-start = ((f32[64,2,128]{2,1,0:T(2,128)}), f32[64,2,128]{2,1,0:T(2,128)S(1)}, u32[]{:S(2)}, u32[]{:S(2)}) async-start(f32[64,2,128]{2,1,0:T(2,128)} %bitcast.136), calls=%async_computation | async-start | bytes 131072 | tf_op jit(solution)/shard_map/all_to_all | solution.py:253
  69.5 6.7 %copy-start.6 = (f32[16,1024]{1,0:T(8,128)S(1)}, f32[16,1024]{1,0:T(8,128)}, u32[]{:S(2)}) copy-start(f32[16,1024]{1,0:T(8,128)} %refs_1_.7) | copy-start | bytes 196612
  69.5 6.7 %copy-start.13 = (f32[16,1024]{1,0:T(8,128)S(1)}, f32[16,1024]{1,0:T(8,128)}, u32[]{:S(2)}) copy-start(f32[16,1024]{1,0:T(8,128)} %param.8) | copy-start | bytes 196612
  69.6 4.0 %copy-start.11 = (f32[64,2,128]{2,1,0:T(2,128)}, f32[64,2,128]{2,1,0:T(2,128)S(1)}, u32[]{:S(2)}) copy-start(f32[64,2,128]{2,1,0:T(2,128)S(1)} %all-to-all-done.refs_0_) | copy-start | bytes 196612
  73.5 40.7 %collective-permute-start.5 = (bf16[256,2048]{0,1:T(8,128)(2,1)}, bf16[256,2048]{0,1:T(8,128)(2,1)}, u32[]{:S(2)}, u32[]{:S(2)}) collective-permute-start(bf16[256,2048]{0,1:T(8,128)(2,1)} %bitcast.29), channel_id=1, source_target_pairs={{0,128},{128,0},{1,129},{129,1},{2,130},{130,2},{3,131},{131,3},{4... | collective-permute-start | bytes 3145736 | tf_op jit(solution)/shard_map/ppermute | solution.py:268
  79.2 24.9 %all-to-all-start.1 = ((f32[64,2,128]{2,1,0:T(2,128)}), f32[64,2,128]{2,1,0:T(2,128)S(1)}, u32[]{:S(2)}, u32[]{:S(2)}) async-start(f32[64,2,128]{2,1,0:T(2,128)} %slab_scan.1), calls=%async_computation.1 | async-start | bytes 131072 | tf_op jit(solution)/shard_map/all_to_all | solution.py:263
  92.3 152.9 %reduce-scatter.5.cloned.1.call-start = ((), (), s32[]{:S(2)}) async-start(), calls=%async_computation.10 | async-start | bytes 4718592 | tf_op jit(solution)/shard_map/reduce_scatter | solution.py:319
  104.2 0.6 copy-start.9
  117.2 6.4 %copy-start.8 = (bf16[256,1024]{1,0:T(8,128)(2,1)S(1)}, bf16[256,1024]{1,0:T(8,128)(2,1)}, u32[]{:S(2)}) copy-start(bf16[256,1024]{1,0:T(8,128)(2,1)} %convert_element_type.99) | copy-start | bytes 1572868
  125.1 14.6 %collective-permute-start.6 = (bf16[256,1024]{1,0:T(8,128)(2,1)}, bf16[256,1024]{1,0:T(8,128)(2,1)}, u32[]{:S(2)}, u32[]{:S(2)}) collective-permute-start(bf16[256,1024]{1,0:T(8,128)(2,1)} %get-tuple-element.55), channel_id=1, source_target_pairs={{0,128},{128,0},{1,129},{129,1},{2,130},{130,2},{3,131},{131,3},{4... | collective-permute-start | bytes 1572872 | tf_op jit(solution)/shard_map/ppermute | solution.py:268
  145.9 22.1 %all-to-all-start.2 = ((f32[64,2,128]{2,1,0:T(2,128)}), f32[64,2,128]{2,1,0:T(2,128)S(1)}, u32[]{:S(2)}, u32[]{:S(2)}) async-start(f32[64,2,128]{2,1,0:T(2,128)} %bitcast.30), calls=%async_computation.2 | async-start | bytes 131072 | tf_op jit(solution)/shard_map/all_to_all | solution.py:253
  168.0 0.6 copy-start.12
  170.3 22.9 %all-to-all-start.3 = ((f32[64,2,128]{2,1,0:T(2,128)}), f32[64,2,128]{2,1,0:T(2,128)S(1)}, u32[]{:S(2)}, u32[]{:S(2)}) async-start(f32[64,2,128]{2,1,0:T(2,128)} %slab_scan_back.1), calls=%async_computation.3 | async-start | bytes 131072 | tf_op jit(solution)/shard_map/all_to_all | solution.py:263
  181.1 77.4 %reduce-scatter.3.cloned.1.call-start = ((), (), s32[]{:S(2)}) async-start(), calls=%async_computation.9 | async-start | bytes 2621440 | tf_op jit(solution)/shard_map/reduce_scatter | solution.py:388
  193.1 7.3 %copy-start.10 = (f32[64,2,128]{2,1,0:T(2,128)}, f32[64,2,128]{2,1,0:T(2,128)S(1)}, u32[]{:S(2)}) copy-start(f32[64,2,128]{2,1,0:T(2,128)S(1)} %all-to-all-done.3) | copy-start | bytes 196612
  208.2 1.8 copy-start
  208.2 1.9 copy-start.5
  208.2 5.5 %copy-start.14 = (f32[16,8,128]{2,1,0:T(8,128)S(1)}, f32[16,8,128]{2,1,0:T(8,128)}, u32[]{:S(2)}) copy-start(f32[16,8,128]{2,1,0:T(8,128)} %get-tuple-element.62) | copy-start | bytes 196612
  208.2 5.5 %copy-start.15 = (f32[16,8,128]{2,1,0:T(8,128)S(1)}, f32[16,8,128]{2,1,0:T(8,128)}, u32[]{:S(2)}) copy-start(f32[16,8,128]{2,1,0:T(8,128)} %get-tuple-element.63) | copy-start | bytes 196612
  210.0 3.3 %copy-start.2 = (bf16[256,1,1024]{2,0,1:T(8,128)(2,1)}, bf16[256,1,1024]{2,0,1:T(8,128)(2,1)S(1)}, u32[]{:S(2)}) copy-start(bf16[256,1,1024]{2,0,1:T(8,128)(2,1)S(1)} %get-tuple-element.79) | copy-start | bytes 1572868
  210.0 3.3 %copy-start.4 = (bf16[256,1,1024]{2,0,1:T(8,128)(2,1)}, bf16[256,1,1024]{2,0,1:T(8,128)(2,1)S(1)}, u32[]{:S(2)}) copy-start(bf16[256,1,1024]{2,0,1:T(8,128)(2,1)S(1)} %get-tuple-element.80) | copy-start | bytes 1572868
  210.0 12.7 %copy-start.1 = (bf16[256,1,1024]{2,0,1:T(8,128)(2,1)S(1)}, bf16[256,1,1024]{2,0,1:T(8,128)(2,1)}, u32[]{:S(2)}) copy-start(bf16[256,1,1024]{2,0,1:T(8,128)(2,1)} %get-tuple-element.89) | copy-start | bytes 1572868
  213.3 17.0 %copy-start.3 = (bf16[256,1,1024]{2,0,1:T(8,128)(2,1)S(1)}, bf16[256,1,1024]{2,0,1:T(8,128)(2,1)}, u32[]{:S(2)}) copy-start(bf16[256,1,1024]{2,0,1:T(8,128)(2,1)} %copy-done.2) | copy-start | bytes 1572868
  214.5 21.5 %all-to-all-start.4 = ((f32[64,8,128]{2,1,0:T(8,128)}), f32[64,8,128]{2,1,0:T(8,128)S(1)}, u32[]{:S(2)}, u32[]{:S(2)}) async-start(f32[64,8,128]{2,1,0:T(8,128)} %maximum_maximum_fusion), calls=%async_computation.5 | async-start | bytes 524288 | tf_op jit(solution)/shard_map/all_to_all | solution.py:335
  224.1 6.2 %collective-permute-start.7 = (bf16[6,3,1024]{2,0,1:T(8,128)(2,1)S(1)}, bf16[6,3,1024]{2,0,1:T(8,128)(2,1)S(1)}, u32[]{:S(2)}, u32[]{:S(2)}) collective-permute-start(bf16[6,3,1024]{2,0,1:T(8,128)(2,1)S(1)} %slice.134), channel_id=1, source_target_pairs={{4,0},{8,4},{12,8},{16,12},{20,16},{24,20},{28,24},{32,28},{36,32}... | collective-permute-start | bytes 110600 | tf_op jit(solution)/shard_map/ppermute | solution.py:303
  236.8 21.7 %all-to-all-start.5 = ((f32[64,8,128]{2,1,0:T(8,128)}), f32[64,8,128]{2,1,0:T(8,128)S(1)}, u32[]{:S(2)}, u32[]{:S(2)}) async-start(f32[64,8,128]{2,1,0:T(8,128)} %broadcast_in_dim.14), calls=%async_computation.6 | async-start | bytes 524288 | tf_op jit(solution)/shard_map/all_to_all | solution.py:338
  247.0 13.6 %collective-permute-start.8 = (bf16[64,1024]{1,0:T(8,128)(2,1)}, bf16[64,1024]{1,0:T(8,128)(2,1)S(1)}, u32[]{:S(2)}, u32[]{:S(2)}) collective-permute-start(bf16[64,1024]{1,0:T(8,128)(2,1)} %get-tuple-element.90), channel_id=1, source_target_pairs={{0,96},{32,0},{64,32},{96,64},{1,97},{33,1},{65,33},{97,65},{2,98}... | collective-permute-start | bytes 393224 | tf_op jit(solution)/shard_map/ppermute | solution.py:268
  249.8 10.9 %collective-permute-start.10 = (bf16[64,1024]{1,0:T(8,128)(2,1)}, bf16[64,1024]{1,0:T(8,128)(2,1)}, u32[]{:S(2)}, u32[]{:S(2)}) collective-permute-start(bf16[64,1024]{1,0:T(8,128)(2,1)} %get-tuple-element.91), channel_id=1, source_target_pairs={{0,32},{32,64},{64,96},{96,0},{1,33},{33,65},{65,97},{97,1},{2,34}... | collective-permute-start | bytes 393224 | tf_op jit(solution)/shard_map/ppermute | solution.py:268
  249.8 12.7 %copy-start.7 = (f32[16,1024]{1,0:T(8,128)S(1)}, f32[16,1024]{1,0:T(8,128)}, u32[]{:S(2)}) copy-start(f32[16,1024]{1,0:T(8,128)} %refs_1_.7) | copy-start | bytes 196612
  249.8 10.8 %collective-permute-start.9 = (bf16[64,1024]{1,0:T(8,128)(2,1)S(1)}, bf16[64,1024]{1,0:T(8,128)(2,1)}, u32[]{:S(2)}, u32[]{:S(2)}) collective-permute-start(bf16[64,1024]{1,0:T(8,128)(2,1)S(1)} %get-tuple-element.92), channel_id=1, source_target_pairs={{0,64},{32,96},{64,0},{96,32},{1,65},{33,97},{65,1},{97,33},{2,66}... | collective-permute-start | bytes 393224 | tf_op jit(solution)/shard_map/ppermute | solution.py:268
Sparse Core Ops, SparseCore 0:
  16.0 100.7 all-gather.1
  146.1 54.6 reduce-scatter.4
  203.3 33.7 reduce-scatter.2
